TPU v7x, 128 devices: a whole 4x4x4 slice. The times are simulated.
128 devices in a mesh: area: 32 (over z, x, core), harm: 4 (over y).
Axes of the slice: x: 4, y: 4, z: 4, core: 2. Of those that a mesh axis runs over, the one named last changes fastest.
Arguments:
- volt: float32 [2, 32, 28, 32, 768], P(None, 'area', 'harm'), may hold values from -3 to 3
- inject: float32 [2, 32, 28, 32, 768], P(None, 'area', 'harm'), may hold values from -6 to 6
- zinv: bfloat16 [2, 32, 28, 768, 768], P(None, 'area', 'harm')
- dev_bus: int32 [32, 2048], P('area'), may hold values from 0 to 767
- dev_count: int32 [32], P('area'), may hold values from 1 to 2048, 32768 in all
- dev_cond: float32 [32, 2048], P('area'), may hold values from 0.1 to 1
- dev_sat: float32 [32, 2048], P('area'), may hold values from 0.2 to 2
- tie_bus: int32 [32, 256], P('area'), may hold values from 0 to 127
- tie_area: int32 [32, 256, 1], P('area'), may hold values from 0 to 31; in each aligned block of 256 rows (0 to 255, 256 to 511, ..., all dimensions but the last counted through in order) at most 16 rows name the same one
- tie_far: int32 [32, 256], P('area'), may hold values from 0 to 127
- tie_res: float32 [32, 256], P('area'), may hold values from 0.5 to 2
- tie_reac: float32 [32, 256], P('area'), may hold values from 0.01 to 0.1
Outputs:
- volt_next: float32 [2, 32, 28, 32, 768], P(None, 'area', 'harm')
Inputs may be any that keep to these rules, and one draw needn't show every extreme that they name: `dev_count`: slot k of an area holds an inverter exactly when k is below its count; the counts sum to 32768 and some area has exactly 2048 inverters. `tie_area`: in one area's list no area is named more than 16 times, and in some list some area is named exactly 16 times; every area is named in some list; a list may name its own area.
All inputs are finite; a program needn't handle non-finite values. No bound on the sum of `dev_count` on one device may be relied on, other than what follows from the above.
Results may differ from a plain program's by a relative error of at most 0.0029.
Values sent between devices are 32-bit elements; how exact they have to be, the bound alone decides.
A program may use at most 128 MiB of HBM per device.

v0:
```python
import math

import jax
import jax.numpy as jnp
from jax import lax
from jax.sharding import PartitionSpec as P

NB = 768
NBD = 128
H = 28
TS = 512
CAP = 2048
SCEN = 32


HIGH = lax.Precision.HIGHEST


def phase_table(first_row, row_count):
    sample_ids = jnp.arange(TS, dtype=jnp.int32)[:, None]
    orders = 2 * (first_row + jnp.arange(row_count, dtype=jnp.int32)) + 1
    phase_turns = sample_ids * orders[None, :] % TS
    angles = phase_turns.astype(jnp.float32) * (2.0 * math.pi / TS)
    return (jnp.cos(angles), jnp.sin(angles))


def slot_currents(all_harm, first_slot, slot_count, dev_bus, dev_count, dev_cond, dev_sat):
    cosine_table, sine_table = phase_table(0, H)
    dev_buses = lax.dynamic_slice_in_dim(dev_bus[0], first_slot, slot_count)
    cond_part = lax.dynamic_slice_in_dim(dev_cond[0], first_slot, slot_count)
    sat_part = lax.dynamic_slice_in_dim(dev_sat[0], first_slot, slot_count)
    live_slot = (first_slot + jnp.arange(slot_count, dtype=jnp.int32) < dev_count[0]).astype(
        jnp.float32
    )
    dev_volt = jnp.take(all_harm, dev_buses, axis=3)
    waveform = jnp.einsum("th,hsk->tsk", cosine_table, dev_volt[0], precision=HIGH) - jnp.einsum(
        "th,hsk->tsk", sine_table, dev_volt[1], precision=HIGH
    )
    current = cond_part * live_slot * waveform + sat_part * live_slot * jnp.tanh(2.0 * waveform)
    onehot = (dev_buses[:, None] == jnp.arange(NB, dtype=jnp.int32)[None, :]).astype(jnp.float32)
    return (current, onehot)


def project_orders(current, onehot, first_row, row_count):
    row_cos, row_sin = phase_table(first_row, row_count)
    harm_real = 2.0 / TS * jnp.einsum("th,tsk->hsk", row_cos, current, precision=HIGH)
    harm_imag = -(2.0 / TS) * jnp.einsum("th,tsk->hsk", row_sin, current, precision=HIGH)
    bus_real = jnp.einsum("hsk,kb->hsb", harm_real, onehot, precision=HIGH)
    bus_imag = jnp.einsum("hsk,kb->hsb", harm_imag, onehot, precision=HIGH)
    return jnp.stack([bus_real, bus_imag], axis=1)


def per_device(
    volt,
    inject,
    zinv,
    dev_bus,
    dev_count,
    dev_cond,
    dev_sat,
    tie_bus,
    tie_area,
    tie_far,
    tie_res,
    tie_reac,
):
    h_local = volt.shape[2]
    harm_index = lax.axis_index("harm")
    rank_count = lax.axis_size("harm")
    slot_count = CAP // rank_count
    all_harm = lax.all_gather(volt, "harm", axis=2, tiled=True)[:, 0]
    current, onehot = slot_currents(
        all_harm, harm_index * slot_count, slot_count, dev_bus, dev_count, dev_cond, dev_sat
    )
    bus_current = lax.psum_scatter(
        project_orders(current, onehot, jnp.int32(0), h_local * lax.axis_size("harm")),
        "harm",
        scatter_dimension=0,
        tiled=True,
    )
    bus_current = jnp.moveaxis(bus_current, 1, 0)
    edge_block = volt[..., :NBD]
    targets = tie_area[0, :, 0]
    far_bus = tie_far[0]
    gathered = lax.all_gather(edge_block, "area", axis=1, tiled=True)
    far_volt = gathered[:, targets, :, :, far_bus]
    orders = (2 * (harm_index * h_local + jnp.arange(h_local, dtype=jnp.int32)) + 1).astype(
        jnp.float32
    )
    resist = tie_res[0][:, None]
    reactance = tie_reac[0][:, None] * orders[None, :]
    denominator = resist * resist + reactance * reactance
    adm_real = (resist / denominator)[:, :, None]
    adm_imag = (-reactance / denominator)[:, :, None]
    tie_real = adm_real * far_volt[:, 0] - adm_imag * far_volt[:, 1]
    tie_imag = adm_real * far_volt[:, 1] + adm_imag * far_volt[:, 0]
    tie_onehot = (tie_bus[0][:, None] == jnp.arange(NBD, dtype=jnp.int32)[None, :]).astype(
        jnp.float32
    )
    tie_real_sum = jnp.einsum("ths,tb->hsb", tie_real, tie_onehot, precision=HIGH)
    tie_imag_sum = jnp.einsum("ths,tb->hsb", tie_imag, tie_onehot, precision=HIGH)
    padding = jnp.zeros((h_local, SCEN, NB - NBD), jnp.float32)
    rhs_real = (
        inject[0, 0] + bus_current[0] + jnp.concatenate([tie_real_sum, padding], axis=2)
    ).astype(jnp.bfloat16)
    rhs_imag = (
        inject[1, 0] + bus_current[1] + jnp.concatenate([tie_imag_sum, padding], axis=2)
    ).astype(jnp.bfloat16)
    zinv_real = zinv[0, 0]
    zinv_imag = zinv[1, 0]
    next_real = jnp.einsum(
        "hij,hsj->hsi", zinv_real, rhs_real, preferred_element_type=jnp.float32
    ) - jnp.einsum("hij,hsj->hsi", zinv_imag, rhs_imag, preferred_element_type=jnp.float32)
    next_imag = jnp.einsum(
        "hij,hsj->hsi", zinv_real, rhs_imag, preferred_element_type=jnp.float32
    ) + jnp.einsum("hij,hsj->hsi", zinv_imag, rhs_real, preferred_element_type=jnp.float32)
    return jnp.stack([next_real, next_imag])[:, None]


def solution(mesh):
    in_specs = (
        P(None, "area", "harm", None, None),
        P(None, "area", "harm", None, None),
        P(None, "area", "harm", None, None),
        P("area", None),
        P("area"),
        P("area", None),
        P("area", None),
        P("area", None),
        P("area", None, None),
        P("area", None),
        P("area", None),
        P("area", None),
    )
    out_specs = P(None, "area", "harm", None, None)
    return jax.shard_map(
        per_device, mesh=mesh, in_specs=in_specs, out_specs=out_specs, check_vma=False
    )
```

profile of v0, /device:TPU:1, one launch (start us, length us, event | category | flops | bytes accessed | tf_op | source)
XLA Modules:
  0.0 491.3 jit_solution(15675334756705943459)
XLA Ops:
  7.4 2.5 copy.40
  12.1 60.1 %all-gather.3.cloned.1.call-done = f32[2,1,28,32,768]{4,3,1,0,2:T(8,128)} async-done(((f32[2,1,7,32,768]{4,3,1,0,2:T(8,128)}), f32[2,1,28,32,768]{4,3,1,0,2:T(8,128)}) %all-gather.3.cloned.1.call-update) | async-done | bytes 5505040 | tf_op jit(solution)/shard_map/all_gather | solution.py:71
  72.2 26.1 %copy.41 = f32[2,1,28,32,768]{3,0,4,2,1:T(2,128)} copy(f32[2,1,28,32,768]{4,3,1,0,2:T(8,128)} %all-gather.3.cloned.1.call-done) | data formatting | bytes 11010048 | tf_op jit(solution)/shard_map/all_gather | solution.py:71
  98.4 41.9 %gather_fusion = f32[512,2,28,32]{3,1,2,0:T(2,128)} fusion(f32[2,28,32,768]{2,0,3,1:T(2,128)} %bitcast.129, s32[1024]{0:T(1024)S(1)} %pad_clamp_fusion), kind=kCustom, calls=%fused_computation | custom fusion | bytes 7342080 | tf_op jit(solution)/shard_map/jit(_take)/gather | solution.py:35
  140.2 15.4 %copy.42 = f32[512,2,28,32]{0,2,3,1:T(8,128)} copy(f32[512,2,28,32]{3,1,2,0:T(2,128)} %gather_fusion) | data formatting | bytes 7340032 | tf_op jit(solution)/shard_map/jit(_take)/gather | solution.py:35
  155.6 2.7 select_bitcast_fusion
  158.4 31.7 %fusion.12 = f32[512,32,512]{2,0,1:T(8,128)} fusion(f32[2,28,32,512]{3,1,2,0:T(8,128)S(1)} %select_bitcast_fusion, s32[28]{0:T(128)S(1)} %multiply_add_fusion.1), kind=kOutput, calls=%fused_computation.19 | convolution fusion | flops 2818772992 | bytes 35652096 | tf_op jit(solution)/shard_map/th,hsk->tsk/dot_general | solution.py:36
  190.0 39.6 %multiply_add_fusion = f32[512,32,512]{2,0,1:T(8,128)} fusion(f32[512,32,512]{2,0,1:T(8,128)} %fusion.12, f32[512]{0:T(512)S(1)} %get-tuple-element.13, f32[512]{0:T(512)S(1)} %get-tuple-element.14, f32[2,28,32,512]{3,1,2,0:T(8,128)S(1)} %select_bitcast_fusion, s32[28]{0:T(128)S(1)} %multiply_add_fusion.1), kind=kOutput, calls=%fused_computation.2 | convolution fusion | flops 2860716032 | bytes 69210624 | tf_op jit(solution)/shard_map/th,hsk->tsk/dot_general | solution.py:36
  229.7 24.4 %convolution_multiply_fusion.1 = f32[28,32,512]{2,0,1:T(8,128)S(1)} fusion(f32[512,32,512]{2,0,1:T(8,128)} %multiply_add_fusion, s32[28]{0:T(128)S(1)} %multiply_add_fusion.1), kind=kOutput, calls=%fused_computation.27 | convolution fusion | flops 2819231744 | bytes 35389552 | tf_op jit(solution)/shard_map/th,tsk->hsk/dot_general | solution.py:46
  254.0 24.8 %convolution_multiply_fusion = f32[28,32,512]{2,0,1:T(8,128)S(1)} fusion(f32[512,32,512]{2,0,1:T(8,128)} %multiply_add_fusion, s32[28]{0:T(128)S(1)} %multiply_add_fusion.1), kind=kOutput, calls=%fused_computation.26 | convolution fusion | flops 2819231744 | bytes 35389552 | tf_op jit(solution)/shard_map/th,tsk->hsk/dot_general | solution.py:47
  278.9 3.7 fusion.17
  282.6 3.7 fusion.20
  286.3 2.8 pad_maximum_fusion
  289.3 1.6 slice.53
  292.5 111.5 %all-reduce.5.cloned.1.call-done = f32[28,2,32,768]{3,2,0,1:T(8,128)} async-done(((f32[28,2,32,768]{3,2,0,1:T(8,128)}), f32[28,2,32,768]{3,2,0,1:T(8,128)}) %all-reduce.5.cloned.1.call-update) | async-done | bytes 5505040
  405.4 35.2 %copy.46 = f32[2,32,7,32,128]{3,0,4,2,1:T(2,128)} copy(f32[2,32,7,32,128]{4,3,2,0,1:T(8,128)} %all-gather.5.cloned.1.call-done) | data formatting | bytes 14680064 | tf_op jit(solution)/shard_map/all_gather | solution.py:85
  440.6 12.7 %gather_fusion.1 = f32[256,2,7,32]{3,1,2,0:T(2,128)S(1)} fusion(f32[2,32,7,32,128]{3,0,4,2,1:T(2,128)} %copy.46, s32[256]{0:T(256)S(1)} %bitcast.130), kind=kCustom, calls=%fused_computation.1 | custom fusion | bytes 919552 | tf_op jit(solution)/shard_map/gather | solution.py:86
  453.3 2.7 fusion.103
  456.0 2.4 copy.47
  458.4 2.3 copy.48
  461.7 6.2 %fusion.2 = f32[7,32,768]{2,1,0:T(8,128)S(1)} fusion(bf16[7,32,768]{2,1,0:T(8,128)(2,1)S(1)} %get-tuple-element.7, bf16[2,1,7,768,768]{4,3,2,1,0:T(8,128)(2,1)} %param.14), kind=kOutput, calls=%fused_computation.5 | convolution fusion | flops 264241152 | bytes 9289728 | tf_op jit(solution)/shard_map/hij,hsj->hsi/dot_general | solution.py:113
  467.8 6.0 %fusion = f32[7,32,768]{2,1,0:T(8,128)S(1)} fusion(bf16[7,32,768]{2,1,0:T(8,128)(2,1)S(1)} %get-tuple-element.8, bf16[2,1,7,768,768]{4,3,2,1,0:T(8,128)(2,1)} %param.14), kind=kOutput, calls=%fused_computation.3 | convolution fusion | flops 264241152 | bytes 9289728 | tf_op jit(solution)/shard_map/hij,hsj->hsi/dot_general | solution.py:116
  473.9 6.0 %fusion.29 = f32[1,7,32,768]{3,2,1,0:T(8,128)S(1)} fusion(f32[7,32,768]{2,1,0:T(8,128)S(1)} %fusion.2, bf16[7,32,768]{2,1,0:T(8,128)(2,1)S(1)} %get-tuple-element.8, bf16[2,1,7,768,768]{4,3,2,1,0:T(8,128)(2,1)} %param.14), kind=kOutput, calls=%fused_computation.33 | convolution fusion | flops 264413184 | bytes 9977856 | tf_op jit(solution)/shard_map/hij,hsj->hsi/dot_general | solution.py:111
  480.0 2.5 fusion.35
  (51 shorter events, 5.9 us)
Async XLA Ops:
  7.4 3.3 copy-start
  7.4 64.9 %all-gather.3.cloned.1.call-start = ((), (), s32[]{:S(2)}) async-start(), calls=%async_computation | async-start | bytes 6881280 | tf_op jit(solution)/shard_map/all_gather | solution.py:71
  9.9 394.0 %all-reduce.5.cloned.1.call-start = ((), (), s32[]{:S(2)}) async-start(), calls=%async_computation.2 | async-start | bytes 11010048
  289.2 1.8 copy-start.3
  289.2 1.8 copy-start.8
  289.2 3.2 copy-start.5
  289.2 3.2 copy-start.6
  289.2 3.2 copy-start.7
  289.2 116.2 %all-gather.5.cloned.1.call-start = ((), (), s32[]{:S(2)}) async-start(), calls=%async_computation.1 | async-start | bytes 7569408 | tf_op jit(solution)/shard_map/all_gather | solution.py:85
  440.6 20.1 %copy-start.4 = (s32[1,256]{1,0:T(1,128)S(1)}, s32[1,256]{1,0:T(1,128)}, u32[]{:S(2)}) copy-start(s32[1,256]{1,0:T(1,128)} %param.19) | copy-start | bytes 3076
  456.0 5.4 %copy-start.2 = (f32[2,1,7,32,768]{4,3,2,1,0:T(8,128)S(1)}, f32[2,1,7,32,768]{4,3,2,1,0:T(8,128)}, u32[]{:S(2)}) copy-start(f32[2,1,7,32,768]{4,3,2,1,0:T(8,128)} %param.13) | copy-start | bytes 4128772
  461.1 18.8 %slice-start = ((s8[16515072]{0:T(1024)(128)(4,1)}), s8[4194304]{0:T(1024)(128)(4,1)S(1)}, s32[]{:S(2)}) async-start(s8[16515072]{0:T(1024)(128)(4,1)} %bitcast.127), calls=%async_computation.3 | async-start | bytes 8388608
  461.7 18.3 %slice-start.1 = ((s8[16515072]{0:T(1024)(128)(4,1)}), s8[4194304]{0:T(1024)(128)(4,1)S(1)}, s32[]{:S(2)}) async-start(s8[16515072]{0:T(1024)(128)(4,1)} %bitcast.127), calls=%async_computation.4 | async-start | bytes 8388608
  467.8 12.1 %slice-start.2 = ((s8[16515072]{0:T(1024)(128)(4,1)}), s8[4194304]{0:T(1024)(128)(4,1)S(1)}, s32[]{:S(2)}) async-start(s8[16515072]{0:T(1024)(128)(4,1)} %bitcast.127), calls=%async_computation.5 | async-start | bytes 8388608
  473.9 6.1 %slice-start.3 = ((s8[16515072]{0:T(1024)(128)(4,1)}), s8[3932160]{0:T(1024)(128)(4,1)S(1)}, s32[]{:S(2)}) async-start(s8[16515072]{0:T(1024)(128)(4,1)} %bitcast.127), calls=%async_computation.6 | async-start | bytes 7864320
  473.9 9.8 %copy-start.1 = (f32[1,2048]{1,0:T(1,128)S(1)}, f32[1,2048]{1,0:T(1,128)}, u32[]{:S(2)}) copy-start(f32[1,2048]{1,0:T(1,128)} %param.18) | copy-start | bytes 24580
Sparse Core Ops, SparseCore 0:
  10.1 62.1 all-gather.2
  289.3 114.5 all-reduce.4
Sparse Core Ops, SparseCore 1:
  291.9 51.8 all-gather.4
where the time goes:
time: 500 us; the launch traced here: 491 us
  waiting for transfers between devices  172 us (34%)
  matrix products  149 us (30%)
  local copies, waits for them, and re-layouts  146 us (29%)
  between operations  16.7 us (3%)
  other arithmetic  7.77 us (2%)
    unnamed x4, waiting for transfers between devices  112 us
    all_gather x1, waiting for transfers between devices, per_device(): all_harm = lax.all_gather(volt, 'harm', axis=2, tiled=True)[:, 0]  60.1 us
    gather x2, local copies, waits for them, and re-layouts, slot_currents(): dev_volt = jnp.take(all_harm, dev_buses, axis=3)  57.3 us
    dot_general x1, matrix products, slot_currents(): jnp.einsum('th,hsk->tsk', sine_table, dev_volt[1], precision=HIGH)  39.6 us
    all_gather x1, local copies, waits for them, and re-layouts, per_device(): gathered = lax.all_gather(edge_block, 'area', axis=1, tiled=True)  35.2 us
    dot_general x1, matrix products, slot_currents(): jnp.einsum('th,hsk->tsk', cosine_table, dev_volt[0], precision=HIGH)  31.7 us
    all_gather x1, local copies, waits for them, and re-layouts, per_device(): all_harm = lax.all_gather(volt, 'harm', axis=2, tiled=True)[:, 0]  26.1 us
    dot_general x1, matrix products, project_orders(): jnp.einsum('th,tsk->hsk', row_sin, current, precision=HIGH)  24.8 us
  transfers between devices with their start and end apart: 3, of which 2 were waited for; matrix products, arithmetic and copies ran while one was open for 1% of the time, Pallas kernels for 0%

commit v1 on v0

v1 whole, which is shorter than its diff:
```python
import math

import jax
import jax.numpy as jnp
from jax import lax
from jax.sharding import PartitionSpec as P

NB = 768
NBD = 128
H = 28
TS = 512
HALF = TS // 2
CAP = 2048
SCEN = 32

HIGH = lax.Precision.HIGHEST


def phase_table():
    sample_ids = jnp.arange(HALF, dtype=jnp.int32)[:, None]
    orders = 2 * jnp.arange(H, dtype=jnp.int32) + 1
    phase_turns = sample_ids * orders[None, :] % TS
    angles = phase_turns.astype(jnp.float32) * (2.0 * math.pi / TS)
    return jnp.concatenate([jnp.cos(angles), -jnp.sin(angles)], axis=1)


def per_device(
    volt,
    inject,
    zinv,
    dev_bus,
    dev_count,
    dev_cond,
    dev_sat,
    tie_bus,
    tie_area,
    tie_far,
    tie_res,
    tie_reac,
):
    h_local = volt.shape[2]
    harm_index = lax.axis_index("harm")
    own = volt[:, 0]
    table = phase_table()
    spread = lax.all_to_all(own, "harm", 2, 1, tiled=True)
    s_local = spread.shape[2]
    spread = spread.reshape(2 * H, s_local, NB)
    waveform = jnp.einsum("tc,csb->tsb", table, spread, precision=HIGH)
    shape = jnp.tanh(2.0 * waveform)
    harmonics = (4.0 / TS) * jnp.einsum("tc,tsb->csb", table, shape, precision=HIGH)
    back = lax.all_to_all(
        harmonics.reshape(2, H, s_local, NB), "harm", 1, 2, tiled=True
    )
    live = (jnp.arange(CAP, dtype=jnp.int32) < dev_count[0]).astype(jnp.float32)
    onehot = (dev_bus[0][:, None] == jnp.arange(NB, dtype=jnp.int32)[None, :]).astype(
        jnp.float32
    )
    sums = jnp.einsum(
        "pk,kb->pb", jnp.stack([live * dev_cond[0], live * dev_sat[0]]), onehot, precision=HIGH
    )
    gathered = lax.all_gather(own[..., :NBD], "area", axis=3, tiled=True)
    entry = tie_area[0, :, 0] * NBD + tie_far[0]
    pick = (
        jnp.arange(gathered.shape[3], dtype=jnp.int32)[:, None] == entry[None, :]
    ).astype(jnp.float32)
    far_volt = jnp.einsum("chse,ej->chsj", gathered, pick, precision=HIGH)
    orders = (2 * (harm_index * h_local + jnp.arange(h_local, dtype=jnp.int32)) + 1).astype(
        jnp.float32
    )
    resist = tie_res[0][None, :]
    reactance = tie_reac[0][None, :] * orders[:, None]
    denominator = resist * resist + reactance * reactance
    adm_real = (resist / denominator)[:, None, :]
    adm_imag = (-reactance / denominator)[:, None, :]
    tie_onehot = (tie_bus[0][:, None] == jnp.arange(NBD, dtype=jnp.int32)[None, :]).astype(
        jnp.float32
    )
    tie = jnp.stack(
        [
            adm_real * far_volt[0] - adm_imag * far_volt[1],
            adm_real * far_volt[1] + adm_imag * far_volt[0],
        ]
    )
    tie_sum = jnp.einsum("chsj,jb->chsb", tie, tie_onehot, precision=HIGH)
    tie_sum = jnp.pad(tie_sum, ((0, 0), (0, 0), (0, 0), (0, NB - NBD)))
    rhs = (inject[:, 0] + sums[0] * own + sums[1] * back + tie_sum).astype(jnp.bfloat16)
    both = jnp.concatenate([rhs[0], rhs[1]], axis=1)
    turned = jnp.concatenate([-rhs[1], rhs[0]], axis=1)
    result = jnp.einsum(
        "hij,hsj->hsi", zinv[0, 0], both, preferred_element_type=jnp.float32
    ) + jnp.einsum("hij,hsj->hsi", zinv[1, 0], turned, preferred_element_type=jnp.float32)
    return jnp.stack([result[:, :SCEN], result[:, SCEN:]])[:, None]


def solution(mesh):
    in_specs = (
        P(None, "area", "harm", None, None),
        P(None, "area", "harm", None, None),
        P(None, "area", "harm", None, None),
        P("area", None),
        P("area"),
        P("area", None),
        P("area", None),
        P("area", None),
        P("area", None, None),
        P("area", None),
        P("area", None),
        P("area", None),
    )
    out_specs = P(None, "area", "harm", None, None)
    return jax.shard_map(
        per_device, mesh=mesh, in_specs=in_specs, out_specs=out_specs, check_vma=False
    )
```

time: 500 us -> 100 us (0.20); the launches traced: 491 us -> 99.7 us
  local copies, waits for them, and re-layouts: 146 us -> 8.09 us
  waiting for transfers between devices: 172 us -> 34.3 us
  matrix products: 149 us -> 30.8 us
  starting transfers between devices: 0.09 us -> 8.87 us
    dot_general x12 -> x7, matrix products: 149 us -> 30.8 us  [the longest x1 6.92 us: per_device(): far_volt = jnp.einsum('chse,ej->chsj', gathered, pick, precision=HIGH)]
    unnamed x4 -> x1, waiting for transfers between devices: 112 us -> 0.02 us
    gather x3 -> x0, local copies, waits for them, and re-layouts: 70 us -> none  [the longest x2 57.3 us: slot_currents(): dev_volt = jnp.take(all_harm, dev_buses, axis=3)]
    all_gather x2 -> x0, local copies, waits for them, and re-layouts: 61.4 us -> none  [the longest x1 35.2 us: per_device(): gathered = lax.all_gather(edge_block, 'area', axis=1, tiled=True)]
    all_gather x2 -> x1, waiting for transfers between devices: 60.2 us -> 19.9 us  [per_device(): gathered = lax.all_gather(own[..., :NBD], 'area', axis=3, tiled=True)]
    all_to_all x0 -> x2, waiting for transfers between devices: none -> 14.5 us  [the longest x1 14.5 us: per_device(): spread = lax.all_to_all(own, 'harm', 2, 1, tiled=True)]
    all_to_all x0 -> x2, starting transfers between devices: none -> 8.87 us  [the longest x1 5.14 us: per_device(): spread = lax.all_to_all(own, 'harm', 2, 1, tiled=True)]
    slice x4 -> x2, local copies, waits for them, and re-layouts: 9.02 us -> 1.66 us  [the longest x1 1.63 us: per_device(): gathered = lax.all_gather(own[..., :NBD], 'area', axis=3, tiled=True)]
  transfers between devices with their start and end apart: 3 -> 3, of which waited for: 2 -> 2; matrix products, arithmetic and copies ran while one was open for 1% -> 25% of each run, Pallas kernels for 0% -> 0%
where the time goes in v1:
time: 100 us; the launch traced here: 99.7 us
  waiting for transfers between devices  34.3 us (34%)
  matrix products  30.8 us (31%)
  between operations  14.3 us (14%)
  starting transfers between devices  8.87 us (9%)
  local copies, waits for them, and re-layouts  8.09 us (8%)
  other arithmetic  3.35 us (3%)
    all_gather x1, waiting for transfers between devices, per_device(): gathered = lax.all_gather(own[..., :NBD], 'area', axis=3, tiled=True)  19.9 us
    all_to_all x1, waiting for transfers between devices, per_device(): spread = lax.all_to_all(own, 'harm', 2, 1, tiled=True)  14.5 us
    dot_general x1, matrix products, per_device(): far_volt = jnp.einsum('chse,ej->chsj', gathered, pick, precision=HIGH)  6.92 us
    dot_general x1, matrix products, per_device(): jnp.einsum('hij,hsj->hsi', zinv[0, 0], both, preferred_element_type=jnp.f...  5.97 us
    dot_general x1, matrix products, per_device(): jnp.einsum('hij,hsj->hsi', zinv[1, 0], turned, preferred_element_type=jnp...  5.94 us
    dot_general x1, matrix products, per_device(): waveform = jnp.einsum('tc,csb->tsb', table, spread, precision=HIGH)  5.2 us
    all_to_all x1, starting transfers between devices, per_device(): spread = lax.all_to_all(own, 'harm', 2, 1, tiled=True)  5.14 us
    dot_general x1, matrix products, per_device(): jnp.einsum('tc,tsb->csb', table, shape, precision=HIGH)  4.22 us
  transfers between devices with their start and end apart: 3, of which 2 were waited for; matrix products, arithmetic and copies ran while one was open for 25% of the time, Pallas kernels for 0%

profile of v1, /device:TPU:1, one launch (start us, length us, event | category | flops | bytes accessed | tf_op | source)
XLA Modules:
  0.0 99.7 jit_solution(18321335147718991607)
XLA Ops:
  6.5 1.6 %slice.50 = f32[2,7,32,128]{3,2,1,0:T(8,128)} slice(f32[2,7,32,768]{3,2,1,0:T(8,128)} %bitcast.75), slice={[0:2], [0:7], [0:32], [0:128]} | slice | bytes 458752 | tf_op jit(solution)/shard_map/slice | solution.py:61
  8.2 3.5 %copy.35 = f32[2,7,32,768]{3,0,1,2:T(2,128)} copy(f32[2,7,32,768]{3,2,1,0:T(8,128)} %bitcast.76) | data formatting | bytes 2752512 | tf_op jit(solution)/shard_map/squeeze | solution.py:43
  11.7 5.1 %all-to-all-start = ((f32[2,7,32,768]{3,0,1,2:T(2,128)}), f32[2,7,32,768]{3,0,1,2:T(2,128)S(1)}, u32[]{:S(2)}, u32[]{:S(2)}) async-start(f32[2,7,32,768]{3,0,1,2:T(2,128)} %copy.35), calls=%async_computation | async-start | bytes 2752512 | tf_op jit(solution)/shard_map/all_to_all | solution.py:45
  17.6 2.1 %fusion.9 = f32[2,768]{1,0:T(2,128)S(1)} fusion(s32[2048]{0:T(1024)S(1)} %bitcast.86, f32[1,2048]{1,0:T(1,128)S(1)} %get-tuple-element.17, f32[1,2048]{1,0:T(1,128)S(1)} %get-tuple-element.18), kind=kOutput, calls=%fused_computation.10 | convolution fusion | flops 39325696 | bytes 30720 | tf_op jit(solution)/shard_map/pk,kb->pb/dot_general | solution.py:58
  19.8 0.1 fusion.55
  19.9 0.2 fusion.52
  20.1 14.5 %all-to-all-done = f32[2,7,32,768]{3,0,1,2:T(2,128)S(1)} async-done(((f32[2,7,32,768]{3,0,1,2:T(2,128)}), f32[2,7,32,768]{3,0,1,2:T(2,128)S(1)}, u32[]{:S(2)}, u32[]{:S(2)}) %all-to-all-start) | async-done | bytes 1376288 | tf_op jit(solution)/shard_map/all_to_all | solution.py:45
  34.6 0.1 copy.51
  34.7 0.1 copy.37
  34.8 5.2 %fusion.25 = f32[256,8,768]{2,0,1:T(8,128)S(1)} fusion(f32[56,8,768]{2,1,0:T(8,128)S(1)} %bitcast.80, f32[256,28]{0,1:T(8,128)S(1)} %get-tuple-element.16, f32[256,28]{0,1:T(8,128)S(1)} %get-tuple-element.15), kind=kOutput, calls=%fused_computation.25 | convolution fusion | flops 1056978944 | bytes 7725056 | tf_op jit(solution)/shard_map/tc,csb->tsb/dot_general | solution.py:48
  40.1 4.2 %fusion.16 = f32[56,8,768]{2,0,1:T(8,128)S(1)} fusion(f32[256,8,768]{2,0,1:T(8,128)S(1)} %fusion.25, f32[256,28]{0,1:T(8,128)S(1)} %get-tuple-element.16, f32[256,28]{0,1:T(8,128)S(1)} %get-tuple-element.15), kind=kOutput, calls=%fused_computation.17 | convolution fusion | flops 1058895872 | bytes 7725056 | tf_op jit(solution)/shard_map/tc,tsb->csb/dot_general | solution.py:50
  44.3 0.4 copy.39
  44.7 1.3 %copy.40 = f32[2,28,8,768]{3,2,0,1:T(8,128)} copy(f32[2,28,8,768]{3,2,1,0:T(8,128)S(1)} %bitcast.79) | data formatting | bytes 2752512 | tf_op jit(solution)/shard_map/reshape | solution.py:52
  46.0 3.7 %all-to-all-start.1 = ((f32[2,28,8,768]{3,2,0,1:T(8,128)}), f32[2,28,8,768]{3,2,0,1:T(8,128)S(1)}, u32[]{:S(2)}, u32[]{:S(2)}) async-start(f32[2,28,8,768]{3,2,0,1:T(8,128)} %copy.40), calls=%async_computation.1 | async-start | bytes 2752512 | tf_op jit(solution)/shard_map/all_to_all | solution.py:51
  49.7 19.9 %all-gather.2.cloned.1.call-done = f32[2,7,32,4096]{3,2,1,0:T(8,128)} async-done(((f32[2,7,32,128]{3,2,1,0:T(8,128)}), f32[2,7,32,4096]{3,2,1,0:T(8,128)}) %all-gather.2.cloned.1.call-update) | async-done | bytes 7340048 | tf_op jit(solution)/shard_map/all_gather | solution.py:61
  69.6 6.9 %fusion.27 = f32[2,7,32,256]{3,2,1,0:T(8,128)S(1)} fusion(f32[2,7,32,4096]{3,2,1,0:T(8,128)} %all-gather.2.cloned.1.call-done, s32[256]{0:T(256)S(1)} %bitcast.85), kind=kOutput, calls=%fused_computation.28 | convolution fusion | flops 5638193152 | bytes 7799808 | tf_op jit(solution)/shard_map/chse,ej->chsj/dot_general | solution.py:66
  76.5 0.1 multiply_subtract_fusion
  76.6 0.4 fusion.36
  77.0 0.8 copy-done
  77.9 1.7 %fusion.24 = bf16[2,7,32,768]{3,2,1,0:T(8,128)(2,1)S(1)} fusion(f32[2,7,4,8,768]{4,3,0,1,2:T(8,128)S(1)} %bitcast.77, f32[2,1,7,32,768]{4,3,2,1,0:T(8,128)} %param.13, f32[2,7,32,128]{3,2,1,0:T(8,128)S(1)} %fusion.36, f32[768]{0:T(1024)S(1)} %get-tuple-element.6, f32[768]{0:T(1024)S(1)} %get-tuple-element.5, f32[2,1,7,32,768]{4,3,2,1,0:T(8,128)S(1)} %copy-done), kind=kLoop, calls=%fused_computation.23 | loop fusion | flops 2064384 | bytes 5052416 | tf_op jit(solution)/shard_map/convert_element_type | solution.py:86
  79.7 5.9 %fusion = f32[7,64,768]{2,1,0:T(8,128)S(1)} fusion(bf16[2,1,7,768,768]{4,3,2,1,0:T(8,128)(2,1)} %param.14, bf16[7,32,768]{2,1,0:T(8,128)(2,1)S(1)} %get-tuple-element.10, bf16[7,32,768]{2,1,0:T(8,128)(2,1)S(1)} %fusion.63), kind=kOutput, calls=%fused_computation | convolution fusion | flops 529858560 | bytes 10321920 | tf_op jit(solution)/shard_map/hij,hsj->hsi/dot_general | solution.py:91
  85.6 6.0 %fusion.19 = f32[7,64,768]{2,1,0:T(8,128)S(1)} fusion(f32[7,64,768]{2,1,0:T(8,128)S(1)} %fusion, bf16[2,1,7,768,768]{4,3,2,1,0:T(8,128)(2,1)} %param.14, bf16[7,32,768]{2,1,0:T(8,128)(2,1)S(1)} %get-tuple-element.9, bf16[7,32,768]{2,1,0:T(8,128)(2,1)S(1)} %get-tuple-element.10), kind=kOutput, calls=%fused_computation.18 | convolution fusion | flops 530202624 | bytes 11698176 | tf_op jit(solution)/shard_map/hij,hsj->hsi/dot_general | solution.py:89
  91.6 0.1 slice_bitcast_fusion.1
  91.7 1.2 %maximum_bitcast_fusion = f32[2,1,7,32,768]{4,3,2,1,0:T(8,128)} fusion(f32[1,7,32,768]{3,2,1,0:T(8,128)S(1)} %get-tuple-element.8, f32[1,7,32,768]{3,2,1,0:T(8,128)S(1)} %get-tuple-element.7), kind=kLoop, calls=%fused_computation.19 | loop fusion | flops 344064 | bytes 2752512 | tf_op jit(solution)/shard_map/broadcast_in_dim | solution.py:92
  (28 shorter events, 0.2 us)
Async XLA Ops:
  6.5 63.0 %all-gather.2.cloned.1.call-start = ((), (), s32[]{:S(2)}) async-start(), calls=%async_computation.2 | async-start | bytes 7569408 | tf_op jit(solution)/shard_map/all_gather | solution.py:61
  11.7 5.9 %copy-start.2 = (f32[1,2048]{1,0:T(1,128)S(1)}, f32[1,2048]{1,0:T(1,128)}, u32[]{:S(2)}) copy-start(f32[1,2048]{1,0:T(1,128)} %param.18) | copy-start | bytes 24580
  11.7 5.9 %copy-start.3 = (f32[1,2048]{1,0:T(1,128)S(1)}, f32[1,2048]{1,0:T(1,128)}, u32[]{:S(2)}) copy-start(f32[1,2048]{1,0:T(1,128)} %param.17) | copy-start | bytes 24580
  11.7 5.9 %copy-start.1 = (f32[1,256]{1,0:T(1,128)S(1)}, f32[1,256]{1,0:T(1,128)}, u32[]{:S(2)}) copy-start(f32[1,256]{1,0:T(1,128)} %param.22) | copy-start | bytes 3076
  11.7 5.9 %copy-start.8 = (s32[1,2048]{1,0:T(1,128)S(1)}, s32[1,2048]{1,0:T(1,128)}, u32[]{:S(2)}) copy-start(s32[1,2048]{1,0:T(1,128)} %param.15) | copy-start | bytes 24580
  11.7 22.9 %all-to-all-start = ((f32[2,7,32,768]{3,0,1,2:T(2,128)}), f32[2,7,32,768]{3,0,1,2:T(2,128)S(1)}, u32[]{:S(2)}, u32[]{:S(2)}) async-start(f32[2,7,32,768]{3,0,1,2:T(2,128)} %copy.35), calls=%async_computation | async-start | bytes 2752512 | tf_op jit(solution)/shard_map/all_to_all | solution.py:45
  16.8 2.9 %copy-start.5 = (s32[1,256]{1,0:T(1,128)S(1)}, s32[1,256]{1,0:T(1,128)}, u32[]{:S(2)}) copy-start(s32[1,256]{1,0:T(1,128)} %param.21) | copy-start | bytes 3076
  16.8 3.0 %copy-start.6 = (s32[1,256,1]{1,2,0:T(1,128)S(1)}, s32[1,256,1]{1,2,0:T(1,128)}, u32[]{:S(2)}) copy-start(s32[1,256,1]{1,2,0:T(1,128)} %param.20) | copy-start | bytes 3076
  16.8 3.0 %copy-start.7 = (f32[1,256]{1,0:T(1,128)S(1)}, f32[1,256]{1,0:T(1,128)}, u32[]{:S(2)}) copy-start(f32[1,256]{1,0:T(1,128)} %param.23) | copy-start | bytes 3076
  46.0 31.0 %all-to-all-start.1 = ((f32[2,28,8,768]{3,2,0,1:T(8,128)}), f32[2,28,8,768]{3,2,0,1:T(8,128)S(1)}, u32[]{:S(2)}, u32[]{:S(2)}) async-start(f32[2,28,8,768]{3,2,0,1:T(8,128)} %copy.40), calls=%async_computation.1 | async-start | bytes 2752512 | tf_op jit(solution)/shard_map/all_to_all | solution.py:51
  69.6 7.0 %copy-start.4 = (s32[1,256]{1,0:T(1,128)S(1)}, s32[1,256]{1,0:T(1,128)}, u32[]{:S(2)}) copy-start(s32[1,256]{1,0:T(1,128)} %param.19) | copy-start | bytes 3076
  76.5 1.3 %copy-start = (f32[2,1,7,32,768]{4,3,2,1,0:T(8,128)S(1)}, f32[2,1,7,32,768]{4,3,2,1,0:T(8,128)}, u32[]{:S(2)}) copy-start(f32[2,1,7,32,768]{4,3,2,1,0:T(8,128)} %param.12) | copy-start | bytes 4128772
Sparse Core Ops, SparseCore 0:
  9.5 60.0 all-gather.1

commit v2 on v1

v2 whole, which is shorter than its diff:
```python
import functools
import math

import jax
import jax.numpy as jnp
import numpy as np
from jax import lax
from jax.experimental import pallas as pl
from jax.experimental.pallas import tpu as pltpu
from jax.sharding import PartitionSpec as P

NB = 768
NBD = 128
H = 28
TS = 512
HALF = TS // 2
CAP = 2048
SCEN = 32
PEER_CAP = 16
RANKS = 4
HL = H // RANKS
CH = 2 * HL
ROWS = RANKS * CH
SL = SCEN // RANKS
LANES = 128
CHUNKS = NB // LANES
BLOCK = 256
SIDE = 256

MESH = pl.DeviceIdType.MESH
F32 = jnp.float32
BF16 = jnp.bfloat16


def phase_tables():
    samples = np.arange(HALF)[:, None]
    columns = []
    for rank in range(RANKS):
        orders = 2 * (rank * HL + np.arange(HL))[None, :] + 1
        angles = (samples * orders % TS) * (2.0 * math.pi / TS)
        columns += [np.cos(angles), -np.sin(angles)]
    table = np.concatenate(columns, axis=1)

    def split(values):
        high = values.astype(np.float32).astype(BF16)
        low = (values - high.astype(np.float64)).astype(np.float32).astype(BF16)
        return high, low

    high, low = split(2.0 * table)
    synthesis = np.concatenate([high, high, low], axis=1)
    high, low = split((4.0 / TS) * table.T)
    analysis = np.concatenate([high, low], axis=0)
    return jnp.asarray(synthesis), jnp.asarray(analysis)


def split_two(values):
    high = values.astype(BF16).astype(F32)
    return high, values - high


def dot_rows(left, right):
    return lax.dot_general(
        left, right, (((1,), (1,)), ((), ())), preferred_element_type=F32
    )


def kernel(
    areas,
    ties,
    count_ref,
    volt_h,
    inject_h,
    zinv_h,
    bus_h,
    cond_h,
    sat_h,
    tarea_h,
    tbus_h,
    tfar_h,
    tres_h,
    treac_h,
    synth_h,
    anal_h,
    out_ref,
    volt_v,
    inject_v,
    zinv_v,
    bus_v,
    cond_v,
    sat_v,
    tarea_v,
    tbus_v,
    tfar_v,
    tres_v,
    treac_v,
    synth_v,
    anal_v,
    fwd_v,
    res_v,
    ret_v,
    req_s,
    req_r,
    tie_s,
    tie_r,
    adm_v,
    place_v,
    tie_v,
    load_sem,
    zinv_sem,
    self_sem,
    fs_sem,
    fr_sem,
    bs_sem,
    br_sem,
    qs_sem,
    qr_sem,
    ts_sem,
    tr_sem,
):
    slots = areas * PEER_CAP
    area = lax.axis_index("area")
    rank = lax.axis_index("harm")

    barrier = pltpu.get_barrier_semaphore()
    for step in range(1, RANKS):
        pl.semaphore_signal(
            barrier, inc=1, device_id=(area, (rank + step) % RANKS), device_id_type=MESH
        )

    def greet(step, carry):
        pl.semaphore_signal(
            barrier, inc=1, device_id=((area + step) % areas, rank), device_id_type=MESH
        )
        return carry

    lax.fori_loop(1, areas, greet, 0)

    pairs = [
        (tarea_h, tarea_v),
        (tbus_h, tbus_v),
        (tfar_h, tfar_v),
        (tres_h, tres_v),
        (treac_h, treac_v),
        (volt_h, volt_v),
        (bus_h, bus_v),
        (cond_h, cond_v),
        (sat_h, sat_v),
        (synth_h, synth_v),
        (anal_h, anal_v),
        (inject_h, inject_v),
    ]
    loads = [
        pltpu.make_async_copy(source, target, load_sem.at[i])
        for i, (source, target) in enumerate(pairs)
    ]
    for load in loads:
        load.start()

    def rank_rows(which):
        return pl.ds(which * CH, CH)

    def scenarios(which):
        return pl.ds(pl.multiple_of(which * SL, SL), SL)

    def lanes(chunk):
        return pl.ds(pl.multiple_of(chunk * LANES, LANES), LANES)

    def own_forward(chunk):
        return pltpu.make_async_copy(
            volt_h.at[:, scenarios(rank), lanes(chunk)],
            fwd_v.at[chunk, rank_rows(rank)],
            self_sem.at[chunk],
        )

    for chunk in range(CHUNKS):
        own_forward(chunk).start()

    order = (1, 2, 0)

    def zinv_copy(block):
        return pltpu.make_async_copy(
            zinv_h.at[:, :, pl.ds(block * BLOCK, BLOCK)],
            zinv_v.at[:, :, pl.ds(block * BLOCK, BLOCK)],
            zinv_sem.at[block],
        )

    for block in order:
        zinv_copy(block).start()

    for load in loads[:5]:
        load.wait()
    tie_rows = lax.broadcasted_iota(jnp.int32, (ties, ties), 0)
    tie_cols = lax.broadcasted_iota(jnp.int32, (ties, ties), 1)
    named = jnp.broadcast_to(tarea_v[...], (ties, ties))
    named_column = jnp.sum(
        jnp.where(tie_rows == tie_cols, named, 0), axis=1, keepdims=True
    )
    earlier = jnp.sum(
        jnp.where((named == named_column) & (tie_rows < tie_cols), 1, 0),
        axis=0,
        keepdims=True,
    )
    slot_row = tarea_v[...] * PEER_CAP + earlier
    slot_ids = lax.broadcasted_iota(jnp.int32, (slots, ties), 0)
    placed = jnp.where(slot_row == slot_ids, 1.0, 0.0).astype(BF16)
    bus_ids = lax.broadcasted_iota(jnp.int32, (NBD, ties), 0)
    far_pick = jnp.where(tfar_v[...] == bus_ids, 1.0, 0.0).astype(BF16)
    req_s[...] = dot_rows(placed, far_pick).reshape(areas, PEER_CAP, NBD)

    loads[5].wait()
    pl.semaphore_wait(barrier, RANKS - 1 + areas - 1)

    def forward(chunk, step):
        target = (rank + step) % RANKS
        return pltpu.make_async_remote_copy(
            src_ref=volt_v.at[:, scenarios(target), lanes(chunk)],
            dst_ref=fwd_v.at[chunk, rank_rows(rank)],
            send_sem=fs_sem.at[chunk, step - 1],
            recv_sem=fr_sem.at[chunk, step - 1],
            device_id=(area, target),
            device_id_type=MESH,
        )

    def backward(chunk, step):
        target = (rank + step) % RANKS
        return pltpu.make_async_remote_copy(
            src_ref=res_v.at[chunk, rank_rows(target)],
            dst_ref=ret_v.at[:, scenarios(rank), lanes(chunk)],
            send_sem=bs_sem.at[chunk, step - 1],
            recv_sem=br_sem.at[chunk, step - 1],
            device_id=(area, target),
            device_id_type=MESH,
        )

    def own_backward(chunk):
        return pltpu.make_async_copy(
            res_v.at[chunk, rank_rows(rank)],
            ret_v.at[:, scenarios(rank), lanes(chunk)],
            self_sem.at[CHUNKS + chunk],
        )

    def request(step):
        target = (area + step) % areas
        return pltpu.make_async_remote_copy(
            src_ref=req_s.at[target],
            dst_ref=req_r.at[area],
            send_sem=qs_sem.at[step],
            recv_sem=qr_sem.at[step],
            device_id=(target, rank),
            device_id_type=MESH,
        )

    def answer(step):
        target = (area + step) % areas
        return pltpu.make_async_remote_copy(
            src_ref=tie_s.at[target],
            dst_ref=tie_r.at[area],
            send_sem=ts_sem.at[step],
            recv_sem=tr_sem.at[step],
            device_id=(target, rank),
            device_id_type=MESH,
        )

    def each_area(action):
        def run(step, carry):
            action(step)
            return carry

        lax.fori_loop(1, areas, run, 0)

    def nth(i):
        return (i + 2) % CHUNKS

    def send_forward(i, carry):
        for step in (2, 1, 3):
            forward(nth(i), step).start()
        return carry

    lax.fori_loop(0, CHUNKS, send_forward, 0)
    each_area(lambda step: request(step).start())
    own_request = pltpu.make_async_copy(
        req_s.at[area], req_r.at[area], self_sem.at[2 * CHUNKS]
    )
    own_request.start()

    tie_bus_pick = jnp.where(tbus_v[...] == bus_ids, 1.0, 0.0).astype(BF16)
    place_v[...] = dot_rows(tie_bus_pick, placed).astype(BF16)
    resist_high, resist_low = split_two(tres_v[...])
    react_high, react_low = split_two(treac_v[...])
    line = lax.broadcasted_iota(jnp.int32, (8, ties), 0)
    columns = jnp.where(line == 0, resist_high, jnp.where(line == 1, resist_low, 0.0))
    columns = jnp.where(line == 2, react_high, jnp.where(line == 3, react_low, columns))
    columns = jnp.where(line == 4, 1.0, columns).astype(BF16)
    at_slot = dot_rows(placed, columns)
    resist = at_slot[:, 0:1] + at_slot[:, 1:2] + (1.0 - at_slot[:, 4:5])
    lane_ids = lax.broadcasted_iota(jnp.int32, (1, SIDE), 1)
    orders = (2 * (rank * HL + lane_ids // SCEN) + 1).astype(F32)
    reactance = (at_slot[:, 2:3] + at_slot[:, 3:4]) * orders
    denominator = resist * resist + reactance * reactance
    adm_v[0] = resist / denominator
    adm_v[1] = -reactance / denominator

    for load in loads[6:9]:
        load.wait()
    totals = jnp.zeros((8, NB), F32)
    line = lax.broadcasted_iota(jnp.int32, (8, BLOCK), 0)
    for part in range(CAP // BLOCK):
        here = slice(part * BLOCK, (part + 1) * BLOCK)
        slot = part * BLOCK + lax.broadcasted_iota(jnp.int32, (1, BLOCK), 1)
        live = jnp.where(slot < count_ref[0], 1.0, 0.0)
        rows = []
        for values in (cond_v[:, here], sat_v[:, here]):
            high, rest = split_two(live * values)
            middle, low = split_two(rest)
            rows += [high, middle, low]
        coefficients = jnp.zeros((8, BLOCK), F32)
        for i, row in enumerate(rows):
            coefficients = jnp.where(line == i, row, coefficients)
        bus_rows = lax.broadcasted_iota(jnp.int32, (NB, BLOCK), 0)
        pick = jnp.where(bus_v[:, here] == bus_rows, 1.0, 0.0).astype(BF16)
        totals = totals + dot_rows(coefficients.astype(BF16), pick)
    conductance = totals[0:1] + totals[1:2] + totals[2:3]
    saturation = totals[3:4] + totals[4:5] + totals[5:6]

    for load in loads[9:]:
        load.wait()

    def law(i, carry):
        chunk = nth(i)
        own_forward(chunk).wait()
        for step in range(1, RANKS):
            forward(chunk, step).wait_recv()
        for s in range(0, SL, 2):
            pair = jnp.concatenate(
                [
                    fwd_v[chunk, :, s, :],
                    fwd_v[chunk, :, s + 1, :],
                ],
                axis=1,
            )
            high, low = split_two(pair)
            stacked = jnp.concatenate([high, low, high], axis=0).astype(BF16)
            wave = jnp.dot(synth_v[...], stacked, preferred_element_type=F32)
            shape = jnp.tanh(wave).astype(BF16)
            both = jnp.dot(anal_v[...], shape, preferred_element_type=F32)
            harmonics = both[:ROWS] + both[ROWS:]
            res_v[chunk, :, s, :] = harmonics[:, :LANES]
            res_v[chunk, :, s + 1, :] = harmonics[:, LANES:]
        for step in (2, 1, 3):
            backward(chunk, step).start()
        own_backward(chunk).start()
        return carry

    lax.fori_loop(0, 2, law, 0)

    each_area(lambda step: request(step).wait_recv())
    own_request.wait()
    wanted = req_r[...].reshape(slots, NBD).astype(BF16)
    wanted = jnp.concatenate([wanted, wanted], axis=1)
    for part in range(2):
        edge = volt_v[part * HL : (part + 1) * HL, :, :NBD].reshape(HL * SCEN, NBD)
        high, low = split_two(edge)
        edge = jnp.concatenate([high, low], axis=1).astype(BF16)
        edge = jnp.concatenate(
            [edge, jnp.zeros((SIDE - HL * SCEN, 2 * NBD), BF16)], axis=0
        )
        tie_s[:, :, part * SIDE : (part + 1) * SIDE] = dot_rows(wanted, edge).reshape(
            areas, PEER_CAP, SIDE
        )
    each_area(lambda step: answer(step).start())
    own_answer = pltpu.make_async_copy(
        tie_s.at[area], tie_r.at[area], self_sem.at[2 * CHUNKS + 1]
    )
    own_answer.start()

    lax.fori_loop(2, CHUNKS, law, 0)

    for place, block in enumerate(order):
        zinv_copy(block).wait()
        for chunk in (2 * block, 2 * block + 1):
            own_backward(chunk).wait()
            for step in range(1, RANKS):
                backward(chunk, step).wait_recv()
        if block == 0:
            each_area(lambda step: answer(step).wait_recv())
            own_answer.wait()
            far = tie_r[...].reshape(slots, 2 * SIDE)
            far_real, far_imag = far[:, :SIDE], far[:, SIDE:]
            adm_real, adm_imag = adm_v[0], adm_v[1]
            for part, value in enumerate(
                (
                    adm_real * far_real - adm_imag * far_imag,
                    adm_real * far_imag + adm_imag * far_real,
                )
            ):
                high, low = split_two(value)
                summed = jnp.dot(
                    place_v[...], high.astype(BF16), preferred_element_type=F32
                ) + jnp.dot(place_v[...], low.astype(BF16), preferred_element_type=F32)
                tie_v[part] = summed.T
        here = slice(block * BLOCK, (block + 1) * BLOCK)
        for h in range(HL):
            sides = []
            for part in range(2):
                row = part * HL + h
                value = (
                    inject_v[row, :, here]
                    + conductance[:, here] * volt_v[row, :, here]
                    + saturation[:, here] * ret_v[row, :, here]
                )
                if block == 0:
                    tie = tie_v[part, h * SCEN : (h + 1) * SCEN, :]
                    value = jnp.concatenate(
                        [value[:, :NBD] + tie, value[:, NBD:]], axis=1
                    )
                sides.append(value)
            real, imag = sides
            straight = jnp.concatenate([real, imag], axis=0).astype(BF16)
            turned = jnp.concatenate([-imag, real], axis=0).astype(BF16)
            total = dot_rows(straight, zinv_v[h, :, here]) + dot_rows(
                turned, zinv_v[HL + h, :, here]
            )
            if place == 0:
                out_ref[h] = total[:SCEN]
                out_ref[HL + h] = total[SCEN:]
            else:
                out_ref[h] += total[:SCEN]
                out_ref[HL + h] += total[SCEN:]

    def drain(i, carry):
        for step in range(1, RANKS):
            forward(i, step).wait_send()
            backward(i, step).wait_send()
        return carry

    lax.fori_loop(0, CHUNKS, drain, 0)
    each_area(lambda step: request(step).wait_send())
    each_area(lambda step: answer(step).wait_send())


def per_device(
    volt,
    inject,
    zinv,
    dev_bus,
    dev_count,
    dev_cond,
    dev_sat,
    tie_bus,
    tie_area,
    tie_far,
    tie_res,
    tie_reac,
):
    areas = lax.axis_size("area")
    ties = tie_bus.shape[1]
    slots = areas * PEER_CAP
    synthesis, analysis = phase_tables()
    anywhere = pl.BlockSpec(memory_space=pl.ANY)
    dma = pltpu.SemaphoreType.DMA
    out = pl.pallas_call(
        functools.partial(kernel, areas, ties),
        out_shape=jax.ShapeDtypeStruct((CH, SCEN, NB), F32),
        in_specs=[pl.BlockSpec(memory_space=pltpu.SMEM)] + [anywhere] * 13,
        out_specs=pl.BlockSpec(memory_space=pltpu.VMEM),
        scratch_shapes=[
            pltpu.VMEM((CH, SCEN, NB), F32),
            pltpu.VMEM((CH, SCEN, NB), F32),
            pltpu.VMEM((CH, NB, NB), BF16),
            pltpu.VMEM((1, CAP), jnp.int32),
            pltpu.VMEM((1, CAP), F32),
            pltpu.VMEM((1, CAP), F32),
            pltpu.VMEM((1, ties), jnp.int32),
            pltpu.VMEM((1, ties), jnp.int32),
            pltpu.VMEM((1, ties), jnp.int32),
            pltpu.VMEM((1, ties), F32),
            pltpu.VMEM((1, ties), F32),
            pltpu.VMEM(synthesis.shape, BF16),
            pltpu.VMEM(analysis.shape, BF16),
            pltpu.VMEM((CHUNKS, ROWS, SL, LANES), F32),
            pltpu.VMEM((CHUNKS, ROWS, SL, LANES), F32),
            pltpu.VMEM((CH, SCEN, NB), F32),
            pltpu.VMEM((areas, PEER_CAP, NBD), F32),
            pltpu.VMEM((areas, PEER_CAP, NBD), F32),
            pltpu.VMEM((areas, PEER_CAP, 2 * SIDE), F32),
            pltpu.VMEM((areas, PEER_CAP, 2 * SIDE), F32),
            pltpu.VMEM((2, slots, SIDE), F32),
            pltpu.VMEM((NBD, slots), BF16),
            pltpu.VMEM((2, SIDE, NBD), F32),
            dma((12,)),
            dma((NB // BLOCK,)),
            dma((2 * CHUNKS + 2,)),
            dma((CHUNKS, RANKS - 1)),
            dma((CHUNKS, RANKS - 1)),
            dma((CHUNKS, RANKS - 1)),
            dma((CHUNKS, RANKS - 1)),
            dma((areas,)),
            dma((areas,)),
            dma((areas,)),
            dma((areas,)),
        ],
        compiler_params=pltpu.CompilerParams(
            collective_id=0, has_side_effects=True, vmem_limit_bytes=60 << 20
        ),
        name="sweep",
    )(
        dev_count,
        volt.reshape(CH, SCEN, NB),
        inject.reshape(CH, SCEN, NB),
        zinv.reshape(CH, NB, NB),
        dev_bus,
        dev_cond,
        dev_sat,
        tie_area.reshape(1, ties),
        tie_bus,
        tie_far,
        tie_res,
        tie_reac,
        synthesis,
        analysis,
    )
    return out.reshape(2, 1, HL, SCEN, NB)


def solution(mesh):
    in_specs = (
        P(None, "area", "harm", None, None),
        P(None, "area", "harm", None, None),
        P(None, "area", "harm", None, None),
        P("area", None),
        P("area"),
        P("area", None),
        P("area", None),
        P("area", None),
        P("area", None, None),
        P("area", None),
        P("area", None),
        P("area", None),
    )
    out_specs = P(None, "area", "harm", None, None)
    return jax.shard_map(
        per_device, mesh=mesh, in_specs=in_specs, out_specs=out_specs, check_vma=False
    )
```

time: 100 us -> 50.4 us (0.50)
  Pallas kernels: 0 us -> 47.1 us
  waiting for transfers between devices: 34.3 us -> 0 us
  matrix products: 30.8 us -> 0 us
  between operations: 14.3 us -> 0.66 us
  starting transfers between devices: 8.87 us -> 0 us
  local copies, waits for them, and re-layouts: 8.09 us -> 2.53 us
  other arithmetic: 3.35 us -> 0 us
    pallas_call x0 -> x1, Pallas kernels: none -> 47.1 us  [per_device(): pl.pallas_call(functools.partial(kernel, areas, ties), out_shape=jax.Shap...]
    dot_general x7 -> x0, matrix products: 30.8 us -> none  [the longest x1 6.92 us: per_device(): far_volt = jnp.einsum('chse,ej->chsj', gathered, pick, precision=HIGH)]
    all_gather x1 -> x0, waiting for transfers between devices: 19.9 us -> none  [per_device(): gathered = lax.all_gather(own[..., :NBD], 'area', axis=3, tiled=True)]
    all_to_all x2 -> x0, waiting for transfers between devices: 14.5 us -> none  [the longest x1 14.5 us: per_device(): spread = lax.all_to_all(own, 'harm', 2, 1, tiled=True)]
    all_to_all x2 -> x0, starting transfers between devices: 8.87 us -> none  [the longest x1 5.14 us: per_device(): spread = lax.all_to_all(own, 'harm', 2, 1, tiled=True)]
    squeeze x2 -> x0, local copies, waits for them, and re-layouts: 3.53 us -> none  [the longest x1 3.48 us: per_device(): own = volt[:, 0]]
    convert_element_type x2 -> x0, other arithmetic: 1.74 us -> none  [the longest x1 1.73 us: per_device(): (inject[:, 0] + sums[0] * own + sums[1] * back + tie_sum).astype(jnp.bflo...]
    unnamed x18 -> x1, local copies, waits for them, and re-layouts: 0.85 us -> 2.53 us
  transfers between devices with their start and end apart: 3 -> 0, of which waited for: 2 -> 0; matrix products, arithmetic and copies ran while one was open for 25% -> 0% of each run, Pallas kernels for 0% -> 0%
where the time goes in v2:
time: 50.4 us; the launch traced here: 50.3 us
  Pallas kernels  47.1 us (93%)
  local copies, waits for them, and re-layouts  2.53 us (5%)
  between operations  0.66 us (1%)
    pallas_call x1, Pallas kernels, per_device(): pl.pallas_call(functools.partial(kernel, areas, ties), out_shape=jax.Shap...  47.1 us
    unnamed x1, local copies, waits for them, and re-layouts  2.53 us

profile of v2, /device:TPU:1, one launch (start us, length us, event | category | flops | bytes accessed | tf_op | source)
XLA Modules:
  0.0 50.3 jit_solution(15289782949358160293)
XLA Ops:
  0.7 47.1 %sweep.1 = f32[14,32,768]{2,1,0:T(8,128)} custom-call(s32[1]{0:T(128)S(6)} %copy.17.count_ref, f32[14,32,768]{2,1,0:T(8,128)} %bitcast.9, f32[14,32,768]{2,1,0:T(8,128)} %bitcast.10, bf16[14,768,768]{2,1,0:T(8,128)(2,1)} %bitcast.7, s32[1,2048]{1,0:T(1,128)} %bus_h.1, f32[1,2048]{1,0:T(1,128)} %cond_h.1, f32[1,2048]{1,0:T(1,128)} %sat_h.1, ...), custom_call_target="tpu_custom_call" | custom-call | tf_op jit(solution)/shard_map/sweep/pallas_call | solution.py:461
  47.7 2.5 %copy.18 = f32[2,1,7,32,768]{4,3,2,1,0:T(8,128)} copy(f32[2,1,7,32,768]{4,3,2,1,0:T(8,128)} %bitcast.8) | data formatting | bytes 2752512

commit v3 on v2

--- a/solution.py
+++ b/solution.py
@@ -67,6 +67,7 @@
 def kernel(
     areas,
     ties,
+    groups,
     count_ref,
     volt_h,
     inject_h,
@@ -116,6 +117,7 @@
     qr_sem,
     ts_sem,
     tr_sem,
+    plane_sem,
 ):
     slots = areas * PEER_CAP
     area = lax.axis_index("area")
@@ -127,13 +129,14 @@
             barrier, inc=1, device_id=(area, (rank + step) % RANKS), device_id_type=MESH
         )
 
-    def greet(step, carry):
-        pl.semaphore_signal(
-            barrier, inc=1, device_id=((area + step) % areas, rank), device_id_type=MESH
-        )
-        return carry
-
-    lax.fori_loop(1, areas, greet, 0)
+    line = areas // groups
+    base = area // line * line
+    for step in range(1, line):
+        peer = base + (area - base + step) % line
+        pl.semaphore_signal(barrier, inc=1, device_id=(peer, rank), device_id_type=MESH)
+    for step in range(1, groups):
+        peer = (area + step * line) % areas
+        pl.semaphore_signal(barrier, inc=1, device_id=(peer, rank), device_id_type=MESH)
 
     pairs = [
         (tarea_h, tarea_v),
@@ -187,33 +190,12 @@
     for block in order:
         zinv_copy(block).start()
 
-    for load in loads[:5]:
-        load.wait()
-    tie_rows = lax.broadcasted_iota(jnp.int32, (ties, ties), 0)
-    tie_cols = lax.broadcasted_iota(jnp.int32, (ties, ties), 1)
-    named = jnp.broadcast_to(tarea_v[...], (ties, ties))
-    named_column = jnp.sum(
-        jnp.where(tie_rows == tie_cols, named, 0), axis=1, keepdims=True
-    )
-    earlier = jnp.sum(
-        jnp.where((named == named_column) & (tie_rows < tie_cols), 1, 0),
-        axis=0,
-        keepdims=True,
-    )
-    slot_row = tarea_v[...] * PEER_CAP + earlier
-    slot_ids = lax.broadcasted_iota(jnp.int32, (slots, ties), 0)
-    placed = jnp.where(slot_row == slot_ids, 1.0, 0.0).astype(BF16)
-    bus_ids = lax.broadcasted_iota(jnp.int32, (NBD, ties), 0)
-    far_pick = jnp.where(tfar_v[...] == bus_ids, 1.0, 0.0).astype(BF16)
-    req_s[...] = dot_rows(placed, far_pick).reshape(areas, PEER_CAP, NBD)
-
-    loads[5].wait()
-    pl.semaphore_wait(barrier, RANKS - 1 + areas - 1)
+    pl.semaphore_wait(barrier, RANKS - 1 + line - 1 + groups - 1)
 
     def forward(chunk, step):
         target = (rank + step) % RANKS
         return pltpu.make_async_remote_copy(
-            src_ref=volt_v.at[:, scenarios(target), lanes(chunk)],
+            src_ref=volt_h.at[:, scenarios(target), lanes(chunk)],
             dst_ref=fwd_v.at[chunk, rank_rows(rank)],
             send_sem=fs_sem.at[chunk, step - 1],
             recv_sem=fr_sem.at[chunk, step - 1],
@@ -277,6 +259,33 @@
         return carry
 
     lax.fori_loop(0, CHUNKS, send_forward, 0)
+    for step in range(1, groups):
+        peer = (area + step * line) % areas
+        pl.semaphore_signal(
+            plane_sem, inc=1, device_id=(peer, rank), device_id_type=MESH
+        )
+
+    for load in loads[:5]:
+        load.wait()
+    tie_rows = lax.broadcasted_iota(jnp.int32, (ties, ties), 0)
+    tie_cols = lax.broadcasted_iota(jnp.int32, (ties, ties), 1)
+    named = jnp.broadcast_to(tarea_v[...], (ties, ties))
+    named_column = jnp.sum(
+        jnp.where(tie_rows == tie_cols, named, 0), axis=1, keepdims=True
+    )
+    earlier = jnp.sum(
+        jnp.where((named == named_column) & (tie_rows < tie_cols), 1, 0),
+        axis=0,
+        keepdims=True,
+    )
+    slot_row = tarea_v[...] * PEER_CAP + earlier
+    slot_ids = lax.broadcasted_iota(jnp.int32, (slots, ties), 0)
+    placed = jnp.where(slot_row == slot_ids, 1.0, 0.0).astype(BF16)
+    bus_ids = lax.broadcasted_iota(jnp.int32, (NBD, ties), 0)
+    far_pick = jnp.where(tfar_v[...] == bus_ids, 1.0, 0.0).astype(BF16)
+    req_s[...] = dot_rows(placed, far_pick).reshape(areas, PEER_CAP, NBD)
+
+    pl.semaphore_wait(plane_sem, groups - 1)
     each_area(lambda step: request(step).start())
     own_request = pltpu.make_async_copy(
         req_s.at[area], req_r.at[area], self_sem.at[2 * CHUNKS]
@@ -287,10 +296,10 @@
     place_v[...] = dot_rows(tie_bus_pick, placed).astype(BF16)
     resist_high, resist_low = split_two(tres_v[...])
     react_high, react_low = split_two(treac_v[...])
-    line = lax.broadcasted_iota(jnp.int32, (8, ties), 0)
-    columns = jnp.where(line == 0, resist_high, jnp.where(line == 1, resist_low, 0.0))
-    columns = jnp.where(line == 2, react_high, jnp.where(line == 3, react_low, columns))
-    columns = jnp.where(line == 4, 1.0, columns).astype(BF16)
+    row_ids = lax.broadcasted_iota(jnp.int32, (8, ties), 0)
+    columns = jnp.where(row_ids == 0, resist_high, jnp.where(row_ids == 1, resist_low, 0.0))
+    columns = jnp.where(row_ids == 2, react_high, jnp.where(row_ids == 3, react_low, columns))
+    columns = jnp.where(row_ids == 4, 1.0, columns).astype(BF16)
     at_slot = dot_rows(placed, columns)
     resist = at_slot[:, 0:1] + at_slot[:, 1:2] + (1.0 - at_slot[:, 4:5])
     lane_ids = lax.broadcasted_iota(jnp.int32, (1, SIDE), 1)
@@ -303,7 +312,7 @@
     for load in loads[6:9]:
         load.wait()
     totals = jnp.zeros((8, NB), F32)
-    line = lax.broadcasted_iota(jnp.int32, (8, BLOCK), 0)
+    row_ids = lax.broadcasted_iota(jnp.int32, (8, BLOCK), 0)
     for part in range(CAP // BLOCK):
         here = slice(part * BLOCK, (part + 1) * BLOCK)
         slot = part * BLOCK + lax.broadcasted_iota(jnp.int32, (1, BLOCK), 1)
@@ -315,7 +324,7 @@
             rows += [high, middle, low]
         coefficients = jnp.zeros((8, BLOCK), F32)
         for i, row in enumerate(rows):
-            coefficients = jnp.where(line == i, row, coefficients)
+            coefficients = jnp.where(row_ids == i, row, coefficients)
         bus_rows = lax.broadcasted_iota(jnp.int32, (NB, BLOCK), 0)
         pick = jnp.where(bus_v[:, here] == bus_rows, 1.0, 0.0).astype(BF16)
         totals = totals + dot_rows(coefficients.astype(BF16), pick)
@@ -324,6 +333,7 @@
 
     for load in loads[9:]:
         load.wait()
+    loads[5].wait()
 
     def law(i, carry):
         chunk = nth(i)
@@ -375,30 +385,31 @@
 
     lax.fori_loop(2, CHUNKS, law, 0)
 
-    for place, block in enumerate(order):
-        zinv_copy(block).wait()
-        for chunk in (2 * block, 2 * block + 1):
-            own_backward(chunk).wait()
-            for step in range(1, RANKS):
-                backward(chunk, step).wait_recv()
-        if block == 0:
-            each_area(lambda step: answer(step).wait_recv())
-            own_answer.wait()
-            far = tie_r[...].reshape(slots, 2 * SIDE)
-            far_real, far_imag = far[:, :SIDE], far[:, SIDE:]
-            adm_real, adm_imag = adm_v[0], adm_v[1]
-            for part, value in enumerate(
-                (
-                    adm_real * far_real - adm_imag * far_imag,
-                    adm_real * far_imag + adm_imag * far_real,
-                )
-            ):
-                high, low = split_two(value)
-                summed = jnp.dot(
-                    place_v[...], high.astype(BF16), preferred_element_type=F32
-                ) + jnp.dot(place_v[...], low.astype(BF16), preferred_element_type=F32)
-                tie_v[part] = summed.T
-        here = slice(block * BLOCK, (block + 1) * BLOCK)
+    def result_in(chunk):
+        own_backward(chunk).wait()
+        for step in range(1, RANKS):
+            backward(chunk, step).wait_recv()
+
+    def gather_ties():
+        each_area(lambda step: answer(step).wait_recv())
+        own_answer.wait()
+        far = tie_r[...].reshape(slots, 2 * SIDE)
+        far_real, far_imag = far[:, :SIDE], far[:, SIDE:]
+        adm_real, adm_imag = adm_v[0], adm_v[1]
+        for part, value in enumerate(
+            (
+                adm_real * far_real - adm_imag * far_imag,
+                adm_real * far_imag + adm_imag * far_real,
+            )
+        ):
+            high, low = split_two(value)
+            summed = jnp.dot(
+                place_v[...], high.astype(BF16), preferred_element_type=F32
+            ) + jnp.dot(place_v[...], low.astype(BF16), preferred_element_type=F32)
+            tie_v[part] = summed.T
+
+    def accumulate(first, chunks, fresh):
+        here = slice(first * LANES, (first + chunks) * LANES)
         for h in range(HL):
             sides = []
             for part in range(2):
@@ -408,11 +419,8 @@
                     + conductance[:, here] * volt_v[row, :, here]
                     + saturation[:, here] * ret_v[row, :, here]
                 )
-                if block == 0:
-                    tie = tie_v[part, h * SCEN : (h + 1) * SCEN, :]
-                    value = jnp.concatenate(
-                        [value[:, :NBD] + tie, value[:, NBD:]], axis=1
-                    )
+                if first == 0:
+                    value = value + tie_v[part, h * SCEN : (h + 1) * SCEN, :]
                 sides.append(value)
             real, imag = sides
             straight = jnp.concatenate([real, imag], axis=0).astype(BF16)
@@ -420,12 +428,24 @@
             total = dot_rows(straight, zinv_v[h, :, here]) + dot_rows(
                 turned, zinv_v[HL + h, :, here]
             )
-            if place == 0:
+            if fresh:
                 out_ref[h] = total[:SCEN]
                 out_ref[HL + h] = total[SCEN:]
             else:
                 out_ref[h] += total[:SCEN]
                 out_ref[HL + h] += total[SCEN:]
+
+    for place, block in enumerate(order[:2]):
+        zinv_copy(block).wait()
+        result_in(2 * block)
+        result_in(2 * block + 1)
+        accumulate(2 * block, 2, place == 0)
+    gather_ties()
+    zinv_copy(0).wait()
+    result_in(0)
+    accumulate(0, 1, False)
+    result_in(1)
+    accumulate(1, 1, False)
 
     def drain(i, carry):
         for step in range(1, RANKS):
@@ -459,8 +479,8 @@
     anywhere = pl.BlockSpec(memory_space=pl.ANY)
     dma = pltpu.SemaphoreType.DMA
     out = pl.pallas_call(
-        functools.partial(kernel, areas, ties),
-        out_shape=jax.ShapeDtypeStruct((CH, SCEN, NB), F32),
+        functools.partial(kernel, areas, ties, 4 if areas > 8 else 2),
+        out_shape=pltpu.VMEM((CH, SCEN, NB), F32),
         in_specs=[pl.BlockSpec(memory_space=pltpu.SMEM)] + [anywhere] * 13,
         out_specs=pl.BlockSpec(memory_space=pltpu.VMEM),
         scratch_shapes=[
@@ -498,6 +518,7 @@
             dma((areas,)),
             dma((areas,)),
             dma((areas,)),
+            pltpu.SemaphoreType.REGULAR,
         ],
         compiler_params=pltpu.CompilerParams(
             collective_id=0, has_side_effects=True, vmem_limit_bytes=60 << 20

time: 50.4 us -> 43 us (0.85)
  Pallas kernels: 47.1 us -> 41 us
  local copies, waits for them, and re-layouts: 2.53 us -> 1.08 us
    pallas_call x1, Pallas kernels: 47.1 us -> 41 us  [per_device(): pl.pallas_call(functools.partial(kernel, areas, ties, 4 if areas > 8 else...]
    unnamed x1, local copies, waits for them, and re-layouts: 2.53 us -> 1.08 us
where the time goes in v3:
time: 43 us; the launch traced here: 42.7 us
  Pallas kernels  41 us (95%)
  local copies, waits for them, and re-layouts  1.08 us (3%)
  between operations  0.66 us (2%)
    pallas_call x1, Pallas kernels, per_device(): pl.pallas_call(functools.partial(kernel, areas, ties, 4 if areas > 8 else...  41 us
    unnamed x1, local copies, waits for them, and re-layouts  1.08 us

profile of v3, /device:TPU:1, one launch (start us, length us, event | category | flops | bytes accessed | tf_op | source)
XLA Modules:
  0.0 42.7 jit_solution(16144440941280823281)
XLA Ops:
  0.7 41.0 %sweep.1 = f32[14,32,768]{2,1,0:T(8,128)S(1)} custom-call(s32[1]{0:T(128)S(6)} %copy.18.count_ref, f32[14,32,768]{2,1,0:T(8,128)} %bitcast.9, f32[14,32,768]{2,1,0:T(8,128)} %bitcast.10, bf16[14,768,768]{2,1,0:T(8,128)(2,1)} %bitcast.8, s32[1,2048]{1,0:T(1,128)} %bus_h.1, f32[1,2048]{1,0:T(1,128)} %cond_h.1, f32[1,2048]{1,0:T(1,128)} %sat_h.1, ...), custom_call_target="tpu_custom_call" | custom-call | tf_op jit(solution)/shard_map/sweep/pallas_call | solution.py:481
  41.6 1.1 %copy.17 = f32[2,1,7,32,768]{4,3,2,1,0:T(8,128)} copy(f32[2,1,7,32,768]{4,3,2,1,0:T(8,128)S(1)} %bitcast.7) | data formatting | bytes 2752512

commit v4 on v3

--- a/solution.py
+++ b/solution.py
@@ -117,6 +117,7 @@
     qr_sem,
     ts_sem,
     tr_sem,
+    entry_sem,
     plane_sem,
 ):
     slots = areas * PEER_CAP
@@ -131,12 +132,119 @@
 
     line = areas // groups
     base = area // line * line
-    for step in range(1, line):
-        peer = base + (area - base + step) % line
-        pl.semaphore_signal(barrier, inc=1, device_id=(peer, rank), device_id_type=MESH)
-    for step in range(1, groups):
-        peer = (area + step * line) % areas
-        pl.semaphore_signal(barrier, inc=1, device_id=(peer, rank), device_id_type=MESH)
+    group = area // line
+    place = area - base
+
+    def greet(semaphore, sign):
+        for step in range(1, line):
+            near = place + sign * step
+
+            @pl.when((near >= 0) & (near < line))
+            def _():
+                pl.semaphore_signal(
+                    semaphore, inc=1, device_id=(base + near, rank), device_id_type=MESH
+                )
+
+        for step in range(1, groups):
+            other = group + sign * step
+
+            @pl.when((other >= 0) & (other < groups))
+            def _():
+                pl.semaphore_signal(
+                    semaphore,
+                    inc=1,
+                    device_id=(other * line + place, rank),
+                    device_id_type=MESH,
+                )
+
+    greet(barrier, 1)
+
+    def rank_rows(which):
+        return pl.ds(which * CH, CH)
+
+    def scenarios(which):
+        return pl.ds(pl.multiple_of(which * SL, SL), SL)
+
+    def lanes(chunk):
+        return pl.ds(pl.multiple_of(chunk * LANES, LANES), LANES)
+
+    def own_forward(chunk):
+        return pltpu.make_async_copy(
+            volt_h.at[:, scenarios(rank), lanes(chunk)],
+            fwd_v.at[chunk, rank_rows(rank)],
+            self_sem.at[chunk],
+        )
+
+    pl.semaphore_wait(barrier, RANKS - 1 + place + group)
+
+    def forward(chunk, step):
+        target = (rank + step) % RANKS
+        return pltpu.make_async_remote_copy(
+            src_ref=volt_h.at[:, scenarios(target), lanes(chunk)],
+            dst_ref=fwd_v.at[chunk, rank_rows(rank)],
+            send_sem=fs_sem.at[chunk, step - 1],
+            recv_sem=fr_sem.at[chunk, step - 1],
+            device_id=(area, target),
+            device_id_type=MESH,
+        )
+
+    def backward(chunk, step):
+        target = (rank + step) % RANKS
+        return pltpu.make_async_remote_copy(
+            src_ref=res_v.at[chunk, rank_rows(target)],
+            dst_ref=ret_v.at[:, scenarios(rank), lanes(chunk)],
+            send_sem=bs_sem.at[chunk, step - 1],
+            recv_sem=br_sem.at[chunk, step - 1],
+            device_id=(area, target),
+            device_id_type=MESH,
+        )
+
+    def own_backward(chunk):
+        return pltpu.make_async_copy(
+            res_v.at[chunk, rank_rows(rank)],
+            ret_v.at[:, scenarios(rank), lanes(chunk)],
+            self_sem.at[CHUNKS + chunk],
+        )
+
+    def request(step):
+        target = (area + step) % areas
+        return pltpu.make_async_remote_copy(
+            src_ref=req_s.at[target],
+            dst_ref=req_r.at[area],
+            send_sem=qs_sem.at[step],
+            recv_sem=qr_sem.at[step],
+            device_id=(target, rank),
+            device_id_type=MESH,
+        )
+
+    def answer(step):
+        target = (area + step) % areas
+        return pltpu.make_async_remote_copy(
+            src_ref=tie_s.at[target],
+            dst_ref=tie_r.at[area],
+            send_sem=ts_sem.at[step],
+            recv_sem=tr_sem.at[step],
+            device_id=(target, rank),
+            device_id_type=MESH,
+        )
+
+    def each_area(action):
+        def run(step, carry):
+            action(step)
+            return carry
+
+        lax.fori_loop(1, areas, run, 0)
+
+    def nth(i):
+        return (i + 2) % CHUNKS
+
+    def send_forward(i, carry):
+        for step in (2, 1, 3):
+            forward(nth(i), step).start()
+        return carry
+
+    lax.fori_loop(0, CHUNKS, send_forward, 0)
+    greet(entry_sem, -1)
 
     pairs = [
         (tarea_h, tarea_v),
@@ -159,22 +267,6 @@
     for load in loads:
         load.start()
 
-    def rank_rows(which):
-        return pl.ds(which * CH, CH)
-
-    def scenarios(which):
-        return pl.ds(pl.multiple_of(which * SL, SL), SL)
-
-    def lanes(chunk):
-        return pl.ds(pl.multiple_of(chunk * LANES, LANES), LANES)
-
-    def own_forward(chunk):
-        return pltpu.make_async_copy(
-            volt_h.at[:, scenarios(rank), lanes(chunk)],
-            fwd_v.at[chunk, rank_rows(rank)],
-            self_sem.at[chunk],
-        )
-
     for chunk in range(CHUNKS):
         own_forward(chunk).start()
 
@@ -189,81 +281,6 @@
 
     for block in order:
         zinv_copy(block).start()
-
-    pl.semaphore_wait(barrier, RANKS - 1 + line - 1 + groups - 1)
-
-    def forward(chunk, step):
-        target = (rank + step) % RANKS
-        return pltpu.make_async_remote_copy(
-            src_ref=volt_h.at[:, scenarios(target), lanes(chunk)],
-            dst_ref=fwd_v.at[chunk, rank_rows(rank)],
-            send_sem=fs_sem.at[chunk, step - 1],
-            recv_sem=fr_sem.at[chunk, step - 1],
-            device_id=(area, target),
-            device_id_type=MESH,
-        )
-
-    def backward(chunk, step):
-        target = (rank + step) % RANKS
-        return pltpu.make_async_remote_copy(
-            src_ref=res_v.at[chunk, rank_rows(target)],
-            dst_ref=ret_v.at[:, scenarios(rank), lanes(chunk)],
-            send_sem=bs_sem.at[chunk, step - 1],
-            recv_sem=br_sem.at[chunk, step - 1],
-            device_id=(area, target),
-            device_id_type=MESH,
-        )
-
-    def own_backward(chunk):
-        return pltpu.make_async_copy(
-            res_v.at[chunk, rank_rows(rank)],
-            ret_v.at[:, scenarios(rank), lanes(chunk)],
-            self_sem.at[CHUNKS + chunk],
-        )
-
-    def request(step):
-        target = (area + step) % areas
-        return pltpu.make_async_remote_copy(
-            src_ref=req_s.at[target],
-            dst_ref=req_r.at[area],
-            send_sem=qs_sem.at[step],
-            recv_sem=qr_sem.at[step],
-            device_id=(target, rank),
-            device_id_type=MESH,
-        )
-
-    def answer(step):
-        target = (area + step) % areas
-        return pltpu.make_async_remote_copy(
-            src_ref=tie_s.at[target],
-            dst_ref=tie_r.at[area],
-            send_sem=ts_sem.at[step],
-            recv_sem=tr_sem.at[step],
-            device_id=(target, rank),
-            device_id_type=MESH,
-        )
-
-    def each_area(action):
-        def run(step, carry):
-            action(step)
-            return carry
-
-        lax.fori_loop(1, areas, run, 0)
-
-    def nth(i):
-        return (i + 2) % CHUNKS
-
-    def send_forward(i, carry):
-        for step in (2, 1, 3):
-            forward(nth(i), step).start()
-        return carry
-
-    lax.fori_loop(0, CHUNKS, send_forward, 0)
-    for step in range(1, groups):
-        peer = (area + step * line) % areas
-        pl.semaphore_signal(
-            plane_sem, inc=1, device_id=(peer, rank), device_id_type=MESH
-        )
 
     for load in loads[:5]:
         load.wait()
@@ -282,9 +299,24 @@
     slot_ids = lax.broadcasted_iota(jnp.int32, (slots, ties), 0)
     placed = jnp.where(slot_row == slot_ids, 1.0, 0.0).astype(BF16)
     bus_ids = lax.broadcasted_iota(jnp.int32, (NBD, ties), 0)
-    far_pick = jnp.where(tfar_v[...] == bus_ids, 1.0, 0.0).astype(BF16)
-    req_s[...] = dot_rows(placed, far_pick).reshape(areas, PEER_CAP, NBD)
-
+    area_ids = lax.broadcasted_iota(jnp.int32, (areas, ties), 0)
+    of_area = jnp.where(tarea_v[...] == area_ids, 1.0, 0.0).astype(BF16)
+    wish = (tfar_v[...] + 1).astype(F32)
+    of_turn = jnp.where(earlier == bus_ids, wish, 0.0).astype(BF16)
+    wishes = dot_rows(of_area, of_turn)
+    req_s[...] = jnp.broadcast_to(wishes[:, None, :], (areas, 8, LANES))
+
+    later = line - 1 - place + groups - 1 - group
+
+    @pl.when(later > 0)
+    def _():
+        pl.semaphore_wait(entry_sem, later)
+
+    for step in range(1, groups):
+        peer = (area + step * line) % areas
+        pl.semaphore_signal(
+            plane_sem, inc=1, device_id=(peer, rank), device_id_type=MESH
+        )
     pl.semaphore_wait(plane_sem, groups - 1)
     each_area(lambda step: request(step).start())
     own_request = pltpu.make_async_copy(
@@ -361,11 +393,21 @@
         own_backward(chunk).start()
         return carry
 
-    lax.fori_loop(0, 2, law, 0)
+    lax.fori_loop(0, 4, law, 0)
 
     each_area(lambda step: request(step).wait_recv())
     own_request.wait()
-    wanted = req_r[...].reshape(slots, NBD).astype(BF16)
+    asked = req_r[:, 0, :].astype(BF16)
+    slot_rows = lax.broadcasted_iota(jnp.int32, (slots, areas), 0) // PEER_CAP
+    slot_cols = lax.broadcasted_iota(jnp.int32, (slots, areas), 1)
+    spread = jnp.where(slot_rows == slot_cols, 1.0, 0.0).astype(BF16)
+    asked = jnp.dot(spread, asked, preferred_element_type=F32)
+    turn_ids = lax.broadcasted_iota(jnp.int32, (slots, LANES), 0) % PEER_CAP
+    far_ids = lax.broadcasted_iota(jnp.int32, (slots, LANES), 1)
+    asked = jnp.sum(
+        jnp.where(turn_ids == far_ids, asked, 0.0), axis=1, keepdims=True
+    ).astype(jnp.int32)
+    wanted = jnp.where(asked == far_ids + 1, 1.0, 0.0).astype(BF16)
     wanted = jnp.concatenate([wanted, wanted], axis=1)
     for part in range(2):
         edge = volt_v[part * HL : (part + 1) * HL, :, :NBD].reshape(HL * SCEN, NBD)
@@ -383,7 +425,7 @@
     )
     own_answer.start()
 
-    lax.fori_loop(2, CHUNKS, law, 0)
+    lax.fori_loop(4, CHUNKS, law, 0)
 
     def result_in(chunk):
         own_backward(chunk).wait()
@@ -435,11 +477,11 @@
                 out_ref[h] += total[:SCEN]
                 out_ref[HL + h] += total[SCEN:]
 
-    for place, block in enumerate(order[:2]):
+    for turn, block in enumerate(order[:2]):
         zinv_copy(block).wait()
         result_in(2 * block)
         result_in(2 * block + 1)
-        accumulate(2 * block, 2, place == 0)
+        accumulate(2 * block, 2, turn == 0)
     gather_ties()
     zinv_copy(0).wait()
     result_in(0)
@@ -500,8 +542,8 @@
             pltpu.VMEM((CHUNKS, ROWS, SL, LANES), F32),
             pltpu.VMEM((CHUNKS, ROWS, SL, LANES), F32),
             pltpu.VMEM((CH, SCEN, NB), F32),
-            pltpu.VMEM((areas, PEER_CAP, NBD), F32),
-            pltpu.VMEM((areas, PEER_CAP, NBD), F32),
+            pltpu.VMEM((areas, 8, LANES), F32),
+            pltpu.VMEM((areas, 8, LANES), F32),
             pltpu.VMEM((areas, PEER_CAP, 2 * SIDE), F32),
             pltpu.VMEM((areas, PEER_CAP, 2 * SIDE), F32),
             pltpu.VMEM((2, slots, SIDE), F32),
@@ -518,6 +560,7 @@
             dma((areas,)),
             dma((areas,)),
             dma((areas,)),
+            pltpu.SemaphoreType.REGULAR,
             pltpu.SemaphoreType.REGULAR,
         ],
         compiler_params=pltpu.CompilerParams(

time: 43 us -> 40.7 us (0.947)
  Pallas kernels: 41 us -> 38.6 us
    pallas_call x1, Pallas kernels: 41 us -> 38.6 us  [per_device(): pl.pallas_call(functools.partial(kernel, areas, ties, 4 if areas > 8 else...]
where the time goes in v4:
time: 40.7 us; the launch traced here: 40.4 us
  Pallas kernels  38.6 us (95%)
  local copies, waits for them, and re-layouts  1.08 us (3%)
  between operations  0.66 us (2%)
    pallas_call x1, Pallas kernels, per_device(): pl.pallas_call(functools.partial(kernel, areas, ties, 4 if areas > 8 else...  38.6 us
    unnamed x1, local copies, waits for them, and re-layouts  1.08 us

profile of v4, /device:TPU:1, one launch (start us, length us, event | category | flops | bytes accessed | tf_op | source)
XLA Modules:
  0.0 40.4 jit_solution(5633213229185595878)
XLA Ops:
  0.7 38.6 %sweep.1 = f32[14,32,768]{2,1,0:T(8,128)S(1)} custom-call(s32[1]{0:T(128)S(6)} %copy.18.count_ref, f32[14,32,768]{2,1,0:T(8,128)} %bitcast.9, f32[14,32,768]{2,1,0:T(8,128)} %bitcast.10, bf16[14,768,768]{2,1,0:T(8,128)(2,1)} %bitcast.8, s32[1,2048]{1,0:T(1,128)} %bus_h.1, f32[1,2048]{1,0:T(1,128)} %cond_h.1, f32[1,2048]{1,0:T(1,128)} %sat_h.1, ...), custom_call_target="tpu_custom_call" | custom-call | tf_op jit(solution)/shard_map/sweep/pallas_call | solution.py:523
  39.3 1.1 %copy.17 = f32[2,1,7,32,768]{4,3,2,1,0:T(8,128)} copy(f32[2,1,7,32,768]{4,3,2,1,0:T(8,128)S(1)} %bitcast.7) | data formatting | bytes 2752512

commit v5 on v4

--- a/solution.py
+++ b/solution.py
@@ -24,6 +24,8 @@
 SL = SCEN // RANKS
 LANES = 128
 CHUNKS = NB // LANES
+LAST = 1
+SPLIT = 8
 BLOCK = 256
 SIDE = 256
 
@@ -48,7 +50,8 @@
 
     high, low = split(2.0 * table)
     synthesis = np.concatenate([high, high, low], axis=1)
-    high, low = split((4.0 / TS) * table.T)
+    turned = table.T.reshape(RANKS, 2, HL, HALF).swapaxes(1, 2).reshape(ROWS, HALF)
+    high, low = split((4.0 / TS) * turned)
     analysis = np.concatenate([high, low], axis=0)
     return jnp.asarray(synthesis), jnp.asarray(analysis)
 
@@ -68,7 +71,7 @@
     areas,
     ties,
     groups,
-    count_ref,
+    count_h,
     volt_h,
     inject_h,
     zinv_h,
@@ -119,6 +122,9 @@
     tr_sem,
     entry_sem,
     plane_sem,
+    count_s,
+    edge_v,
+    edge_sem,
 ):
     slots = areas * PEER_CAP
     area = lax.axis_index("area")
@@ -188,16 +194,29 @@
             device_id_type=MESH,
         )
 
-    def backward(chunk, step):
+    def backward(chunk, step, first=0, count=CH, line=None):
         target = (rank + step) % RANKS
+        line = chunk if line is None else line
         return pltpu.make_async_remote_copy(
-            src_ref=res_v.at[chunk, rank_rows(target)],
-            dst_ref=ret_v.at[:, scenarios(rank), lanes(chunk)],
-            send_sem=bs_sem.at[chunk, step - 1],
-            recv_sem=br_sem.at[chunk, step - 1],
+            src_ref=res_v.at[chunk, pl.ds(target * CH + first, count)],
+            dst_ref=ret_v.at[pl.ds(first, count), scenarios(rank), lanes(chunk)],
+            send_sem=bs_sem.at[line, step - 1],
+            recv_sem=br_sem.at[line, step - 1],
             device_id=(area, target),
             device_id_type=MESH,
         )
+
+    def last_part(part, step):
+        return backward(
+            LAST, step, part * SPLIT, (SPLIT, CH - SPLIT)[part], LAST + part * (CHUNKS - LAST)
+        )
+
+    def each_target(action):
+        for target in range(RANKS):
+
+            @pl.when(rank != target)
+            def _():
+                action((target - rank + RANKS) % RANKS)
 
     def own_backward(chunk):
         return pltpu.make_async_copy(
@@ -259,6 +278,7 @@
         (synth_h, synth_v),
         (anal_h, anal_v),
         (inject_h, inject_v),
+        (count_h, count_s),
     ]
     loads = [
         pltpu.make_async_copy(source, target, load_sem.at[i])
@@ -270,7 +290,7 @@
     for chunk in range(CHUNKS):
         own_forward(chunk).start()
 
-    order = (1, 2, 0)
+    order = (1, 2)
 
     def zinv_copy(block):
         return pltpu.make_async_copy(
@@ -279,8 +299,18 @@
             zinv_sem.at[block],
         )
 
+    def edge_copy(chunk, part):
+        return pltpu.make_async_copy(
+            zinv_h.at[pl.ds(part * HL, HL), :, pl.ds(chunk * LANES, LANES)],
+            edge_v.at[chunk, :, :, pl.ds(part * LANES, LANES)],
+            edge_sem.at[chunk, part],
+        )
+
     for block in order:
         zinv_copy(block).start()
+    for chunk in range(2):
+        for part in range(2):
+            edge_copy(chunk, part).start()
 
     for load in loads[:5]:
         load.wait()
@@ -341,14 +371,14 @@
     adm_v[0] = resist / denominator
     adm_v[1] = -reactance / denominator
 
-    for load in loads[6:9]:
+    for load in loads[6:9] + loads[12:]:
         load.wait()
     totals = jnp.zeros((8, NB), F32)
     row_ids = lax.broadcasted_iota(jnp.int32, (8, BLOCK), 0)
     for part in range(CAP // BLOCK):
         here = slice(part * BLOCK, (part + 1) * BLOCK)
         slot = part * BLOCK + lax.broadcasted_iota(jnp.int32, (1, BLOCK), 1)
-        live = jnp.where(slot < count_ref[0], 1.0, 0.0)
+        live = jnp.where(slot < count_s[0], 1.0, 0.0)
         rows = []
         for values in (cond_v[:, here], sat_v[:, here]):
             high, rest = split_two(live * values)
@@ -363,7 +393,7 @@
     conductance = totals[0:1] + totals[1:2] + totals[2:3]
     saturation = totals[3:4] + totals[4:5] + totals[5:6]
 
-    for load in loads[9:]:
+    for load in loads[9:12]:
         load.wait()
     loads[5].wait()
 
@@ -388,12 +418,21 @@
             harmonics = both[:ROWS] + both[ROWS:]
             res_v[chunk, :, s, :] = harmonics[:, :LANES]
             res_v[chunk, :, s + 1, :] = harmonics[:, LANES:]
-        for step in (2, 1, 3):
-            backward(chunk, step).start()
         own_backward(chunk).start()
+
+        @pl.when(chunk != LAST)
+        def _():
+            for step in (1, 3, 2):
+                backward(chunk, step).start()
+
+        @pl.when(chunk == LAST)
+        def _():
+            each_target(lambda step: last_part(0, step).start())
+            each_target(lambda step: last_part(1, step).start())
+
         return carry
 
-    lax.fori_loop(0, 4, law, 0)
+    lax.fori_loop(0, 3, law, 0)
 
     each_area(lambda step: request(step).wait_recv())
     own_request.wait()
@@ -425,7 +464,7 @@
     )
     own_answer.start()
 
-    lax.fori_loop(4, CHUNKS, law, 0)
+    lax.fori_loop(3, CHUNKS, law, 0)
 
     def result_in(chunk):
         own_backward(chunk).wait()
@@ -450,16 +489,16 @@
             ) + jnp.dot(place_v[...], low.astype(BF16), preferred_element_type=F32)
             tie_v[part] = summed.T
 
-    def accumulate(first, chunks, fresh):
+    def accumulate(first, chunks, fresh, low=0, high=HL):
         here = slice(first * LANES, (first + chunks) * LANES)
-        for h in range(HL):
+        for h in range(low, high):
             sides = []
             for part in range(2):
                 row = part * HL + h
                 value = (
                     inject_v[row, :, here]
                     + conductance[:, here] * volt_v[row, :, here]
-                    + saturation[:, here] * ret_v[row, :, here]
+                    + saturation[:, here] * ret_v[2 * h + part, :, here]
                 )
                 if first == 0:
                     value = value + tie_v[part, h * SCEN : (h + 1) * SCEN, :]
@@ -467,9 +506,14 @@
             real, imag = sides
             straight = jnp.concatenate([real, imag], axis=0).astype(BF16)
             turned = jnp.concatenate([-imag, real], axis=0).astype(BF16)
-            total = dot_rows(straight, zinv_v[h, :, here]) + dot_rows(
-                turned, zinv_v[HL + h, :, here]
-            )
+            if chunks == 1:
+                total = dot_rows(
+                    jnp.concatenate([straight, turned], axis=1), edge_v[first, h]
+                )
+            else:
+                total = dot_rows(straight, zinv_v[h, :, here]) + dot_rows(
+                    turned, zinv_v[HL + h, :, here]
+                )
             if fresh:
                 out_ref[h] = total[:SCEN]
                 out_ref[HL + h] = total[SCEN:]
@@ -477,25 +521,39 @@
                 out_ref[h] += total[:SCEN]
                 out_ref[HL + h] += total[SCEN:]
 
-    for turn, block in enumerate(order[:2]):
+    for turn, block in enumerate(order):
+        if turn == 1:
+            gather_ties()
         zinv_copy(block).wait()
         result_in(2 * block)
         result_in(2 * block + 1)
         accumulate(2 * block, 2, turn == 0)
-    gather_ties()
-    zinv_copy(0).wait()
+    for chunk in range(2):
+        for part in range(2):
+            edge_copy(chunk, part).wait()
     result_in(0)
     accumulate(0, 1, False)
-    result_in(1)
-    accumulate(1, 1, False)
+    own_backward(LAST).wait()
+    for part in range(2):
+        for step in range(1, RANKS):
+            last_part(part, step).wait_recv()
+        middle = SPLIT // 2
+        accumulate(LAST, 1, False, *((0, middle), (middle, HL))[part])
 
     def drain(i, carry):
         for step in range(1, RANKS):
             forward(i, step).wait_send()
-            backward(i, step).wait_send()
+
+            @pl.when(i != LAST)
+            def _():
+                backward(i, step).wait_send()
+
         return carry
 
     lax.fori_loop(0, CHUNKS, drain, 0)
+    for part in range(2):
+        for step in range(1, RANKS):
+            last_part(part, step).wait_send()
     each_area(lambda step: request(step).wait_send())
     each_area(lambda step: answer(step).wait_send())
 
@@ -523,7 +581,7 @@
     out = pl.pallas_call(
         functools.partial(kernel, areas, ties, 4 if areas > 8 else 2),
         out_shape=pltpu.VMEM((CH, SCEN, NB), F32),
-        in_specs=[pl.BlockSpec(memory_space=pltpu.SMEM)] + [anywhere] * 13,
+        in_specs=[anywhere] * 14,
         out_specs=pl.BlockSpec(memory_space=pltpu.VMEM),
         scratch_shapes=[
             pltpu.VMEM((CH, SCEN, NB), F32),
@@ -549,19 +607,22 @@
             pltpu.VMEM((2, slots, SIDE), F32),
             pltpu.VMEM((NBD, slots), BF16),
             pltpu.VMEM((2, SIDE, NBD), F32),
-            dma((12,)),
+            dma((13,)),
             dma((NB // BLOCK,)),
             dma((2 * CHUNKS + 2,)),
             dma((CHUNKS, RANKS - 1)),
             dma((CHUNKS, RANKS - 1)),
-            dma((CHUNKS, RANKS - 1)),
-            dma((CHUNKS, RANKS - 1)),
+            dma((CHUNKS + 1, RANKS - 1)),
+            dma((CHUNKS + 1, RANKS - 1)),
             dma((areas,)),
             dma((areas,)),
             dma((areas,)),
             dma((areas,)),
             pltpu.SemaphoreType.REGULAR,
             pltpu.SemaphoreType.REGULAR,
+            pltpu.SMEM((1,), jnp.int32),
+            pltpu.VMEM((2, HL, NB, 2 * LANES), BF16),
+            dma((2, 2)),
         ],
         compiler_params=pltpu.CompilerParams(
             collective_id=0, has_side_effects=True, vmem_limit_bytes=60 << 20

time: 40.7 us -> 40.3 us (level)
  no operation moved by 1% of the time
where the time goes in v5:
time: 40.3 us; the launch traced here: 40.1 us
  Pallas kernels  38.4 us (95%)
  local copies, waits for them, and re-layouts  1.08 us (3%)
  between operations  0.66 us (2%)
    pallas_call x1, Pallas kernels, per_device(): pl.pallas_call(functools.partial(kernel, areas, ties, 4 if areas > 8 else...  38.4 us
    unnamed x1, local copies, waits for them, and re-layouts  1.08 us

profile of v5, /device:TPU:1, one launch (start us, length us, event | category | flops | bytes accessed | tf_op | source)
XLA Modules:
  0.0 40.1 jit_solution(10398664297058061751)
XLA Ops:
  0.7 38.4 %sweep.1 = f32[14,32,768]{2,1,0:T(8,128)S(1)} custom-call(s32[1]{0:T(128)S(6)} %copy.18.count_h, f32[14,32,768]{2,1,0:T(8,128)} %bitcast.9, f32[14,32,768]{2,1,0:T(8,128)} %bitcast.10, bf16[14,768,768]{2,1,0:T(8,128)(2,1)} %bitcast.8, s32[1,2048]{1,0:T(1,128)} %bus_h.1, f32[1,2048]{1,0:T(1,128)} %cond_h.1, f32[1,2048]{1,0:T(1,128)} %sat_h.1, ...), custom_call_target="tpu_custom_call" | custom-call | tf_op jit(solution)/shard_map/sweep/pallas_call | solution.py:581
  39.0 1.1 %copy.17 = f32[2,1,7,32,768]{4,3,2,1,0:T(8,128)} copy(f32[2,1,7,32,768]{4,3,2,1,0:T(8,128)S(1)} %bitcast.7) | data formatting | bytes 2752512
